TPU v7x, 512 devices: a whole 4x8x8 slice. The times are simulated.
512 devices in a mesh: tm: 64 (over y, z_lo, core), sta: 8 (over x, z_hi).
Axes of the slice: x: 4, y: 8, z: 8 (z_hi: 2, z_lo: 4; z = z_hi * 4 + z_lo), core: 2. Of those that a mesh axis runs over, the one named last changes fastest.
Arguments:
- data: bfloat16 [64, 3, 24576], P('sta', None, 'tm'), as said below
- bank: bfloat16 [64, 8, 64, 3, 150], P('tm', None, 'sta'), may hold values from -6 to 6
- owners: int32 [2], replicated, may hold values from 0 to 63
- moveouts: int32 [2, 8, 64], P(None, None, 'sta'), may hold values from 0 to 64, as said below
Outputs:
- stack: float32 [2, 8, 24576], P(None, 'sta', 'tm')
Inputs may be any that keep to these rules, and one draw needn't show every extreme that they name: `data`: three-component records with amplitudes that vary from station to station and along time. `moveouts`: delays are relative to the earliest arrival: for each template some station has 0 and some other station has 64.
All inputs are finite; a program needn't handle non-finite values.
Results may differ from a plain program's by a relative error of at most 0.0003.
Values may be sent and summed in bfloat16 or wider, within the bound.
No kernel may reach another device: no remote copies, remote signals or barrier semaphores. Data moves between devices by JAX's collectives and lax.ppermute only.
A program may use at most 64 MiB of HBM per device.

v0:
```python
import jax
import jax.numpy as jnp
from jax import lax
from jax.sharding import PartitionSpec as P

MAXM = 64


eps = 1e-06


def passed_along(block, axis, distance):
    devices = range(lax.axis_size(axis))
    route = [(i - distance, i) for i in devices if i - distance in devices]
    return lax.ppermute(block, axis, route)


def correlate(window, batches):
    batch_count, tmpl_count, local_sta, comp_count, span_len = batches.shape
    kernels = jnp.transpose(batches, (2, 0, 1, 3, 4)).reshape(
        local_sta * batch_count * tmpl_count, comp_count, span_len
    )
    records = window.reshape(1, local_sta * comp_count, window.shape[2])
    products = lax.conv_general_dilated(
        records,
        kernels,
        (1,),
        "VALID",
        dimension_numbers=("NCH", "OIH", "NCH"),
        feature_group_count=local_sta,
        preferred_element_type=jnp.float32,
    )
    products = products.reshape(local_sta, batch_count * tmpl_count, products.shape[2])
    squares = jnp.sum(jnp.square(window.astype(jnp.float32)), axis=1)
    energy = lax.reduce_window(squares, 0.0, lax.add, (1, span_len), (1, 1), "VALID") / (
        comp_count * span_len
    )
    tmpl_power = jnp.sum(jnp.square(batches.astype(jnp.float32)), axis=(3, 4)) / (
        comp_count * span_len
    )
    tmpl_power = jnp.transpose(tmpl_power, (2, 0, 1)).reshape(local_sta, batch_count * tmpl_count)
    return products / (
        comp_count
        * span_len
        * jnp.sqrt(tmpl_power + eps)[:, :, None]
        * jnp.sqrt(energy + eps)[None, :, :].transpose(1, 0, 2)
    )


def shift_rows(scores, lag_table, stretch_len):

    def one_row(row, lag_value):
        return lax.dynamic_slice_in_dim(row, lag_value, stretch_len, 0)

    return jax.vmap(jax.vmap(one_row))(scores, lag_table)


def shards(data, bank, owners, moveouts):
    local_sta, comp_count, stretch_len = data.shape
    span_len = bank.shape[-1]
    tmpl_count = bank.shape[1]
    batch_count = owners.shape[0]
    owned_bank = bank[0]
    device_pos = lax.axis_index("tm")
    masked = jnp.stack(
        [
            jnp.where(owners[batch_id] == device_pos, owned_bank.astype(jnp.float32), 0.0)
            for batch_id in range(batch_count)
        ]
    )
    batches = lax.psum(masked, "tm").astype(jnp.bfloat16)
    edge_cells = passed_along(data[:, :, : span_len - 1 + MAXM], "tm", -1)
    scores = correlate(jnp.concatenate([data, edge_cells], axis=2), batches)
    lag_table = jnp.transpose(moveouts, (2, 0, 1)).reshape(local_sta, batch_count * tmpl_count)
    shifted = shift_rows(scores, lag_table, stretch_len)
    partial_sum = jnp.sum(shifted, axis=0).reshape(batch_count, tmpl_count, stretch_len)
    return lax.psum_scatter(partial_sum, "sta", scatter_dimension=1, tiled=True)


def solution(mesh):
    placed = (P("sta", None, "tm"), P("tm", None, "sta", None, None), P(), P(None, None, "sta"))
    return jax.shard_map(
        shards, mesh=mesh, in_specs=placed, out_specs=P(None, "sta", "tm"), check_vma=False
    )
```

profile of v0, /device:TPU:1, one launch (start us, length us, event | category | flops | bytes accessed | tf_op | source)
XLA Modules:
  0.0 790.9 jit_solution(17727927830055742186)
XLA Ops:
  0.7 8.7 %collective-permute-start = (bf16[8,3,213]{2,0,1:T(8,128)(2,1)S(1)}, bf16[8,3,213]{2,0,1:T(8,128)(2,1)S(1)}, u32[]{:S(2)}, u32[]{:S(2)}) collective-permute-start(bf16[8,3,213]{2,0,1:T(8,128)(2,1)S(1)} %slice.9), channel_id=1, source_target_pairs={{8,0},{16,8},{24,16},{32,24},{40,32},{48,40},{56,48},{64,56},{72,6... | collective-permute-start | bytes 30680 | tf_op jit(solution)/shard_map/ppermute | solution.py:15
  13.9 265.2 %all-reduce.2 = bf16[2,8,8,3,150]{4,1,0,3,2:T(8,128)(2,1)S(1)} all-reduce(f32[2,8,8,3,150]{4,1,0,3,2:T(8,128)S(1)} %pad_maximum_fusion), channel_id=1, replica_groups=mesh['tm'=64,'sta'=8] {'tm'}, use_global_device_ids=true, to_apply=%region_0.1 | all-reduce | flops 57600 | bytes 345600 | tf_op jit(solution)/shard_map/psum | solution.py:71
  279.5 2.0 copy.43
  284.1 2.5 copy.42
  286.6 9.1 %reduce_window_sum.9 = f32[8,448]{1,0:T(8,128)S(1)} reduce-window(f32[8,597]{1,0:T(8,128)S(1)} %multiply_reduce_fusion.1, f32[]{:T(128)} %constant.6.clone.1), window={size=1x150}, to_apply=%region_3.4 | reduce-window | flops 534016 | bytes 33444 | tf_op jit(solution)/shard_map/reduce_window_sum | solution.py:35
  296.6 98.9 %fusion.2 = f32[1,8,16,448]{2,0,1,3:T(1,128)S(1)} fusion(bf16[1,8,3,597]{2,0,1,3:T(2,128)(2,1)S(1)} %copy.42, bf16[8,16,3,150]{1,2,0,3:T(4,128)(2,1)} %copy.43), kind=kOutput, calls=%fused_computation.18 | convolution fusion | flops 51609600 | bytes 373232 | tf_op jit(solution)/shard_map/conv_general_dilated | solution.py:24
  397.0 344.8 %while.1 = (s32[]{:T(128)}, f32[8,16,448]{2,1,0:T(8,128)S(1)}, s32[128,3]{0,1:T(4,128)S(1)}, f32[128,384]{1,0:T(8,128)S(1)}, s32[]{:T(128)}, /*index=5*/s32[]{:T(128)}) while((s32[]{:T(128)}, f32[8,16,448]{2,1,0:T(8,128)S(1)}, s32[128,3]{0,1:T(4,128)S(1)}, f32[128,384]{1,0:T(8,128)S(1)}, s32[]{:T(128)}, /*index=5*/s32[]{:T(128)}) %tuple.32), condition=%wide.while_cond, body=%wide.while_body.sunk | while | flops 2 | bytes 6281 | solution.py:53
  400.4 2.0 dynamic-slice_bitcast_fusion.2
  405.8 2.0 dynamic-slice_bitcast_fusion.2
  411.1 2.0 dynamic-slice_bitcast_fusion.2
  416.5 2.0 dynamic-slice_bitcast_fusion.2
  419.2 2.0 dynamic-slice_bitcast_fusion.2
  424.6 2.0 dynamic-slice_bitcast_fusion.2
  430.0 2.0 dynamic-slice_bitcast_fusion.2
  435.4 2.0 dynamic-slice_bitcast_fusion.2
  440.8 2.0 dynamic-slice_bitcast_fusion.2
  446.2 2.0 dynamic-slice_bitcast_fusion.2
  451.6 2.0 dynamic-slice_bitcast_fusion.2
  456.9 2.0 dynamic-slice_bitcast_fusion.2
  462.3 2.0 dynamic-slice_bitcast_fusion.2
  467.7 2.0 dynamic-slice_bitcast_fusion.2
  470.4 2.0 dynamic-slice_bitcast_fusion.2
  475.8 2.0 dynamic-slice_bitcast_fusion.2
  481.2 2.0 dynamic-slice_bitcast_fusion.2
  486.6 2.0 dynamic-slice_bitcast_fusion.2
  492.0 2.0 dynamic-slice_bitcast_fusion.2
  497.4 2.0 dynamic-slice_bitcast_fusion.2
  502.7 2.0 dynamic-slice_bitcast_fusion.2
  508.1 2.0 dynamic-slice_bitcast_fusion.2
  513.5 2.0 dynamic-slice_bitcast_fusion.2
  518.9 2.0 dynamic-slice_bitcast_fusion.2
  521.6 2.0 dynamic-slice_bitcast_fusion.2
  527.0 2.0 dynamic-slice_bitcast_fusion.2
  532.4 2.0 dynamic-slice_bitcast_fusion.2
  537.8 2.0 dynamic-slice_bitcast_fusion.2
  543.2 2.0 dynamic-slice_bitcast_fusion.2
  548.5 2.0 dynamic-slice_bitcast_fusion.2
  553.9 2.0 dynamic-slice_bitcast_fusion.2
  559.3 2.0 dynamic-slice_bitcast_fusion.2
  564.7 2.0 dynamic-slice_bitcast_fusion.2
  570.1 2.0 dynamic-slice_bitcast_fusion.2
  572.8 2.0 dynamic-slice_bitcast_fusion.2
  578.2 2.0 dynamic-slice_bitcast_fusion.2
  583.6 2.0 dynamic-slice_bitcast_fusion.2
  589.0 2.0 dynamic-slice_bitcast_fusion.2
  594.3 2.0 dynamic-slice_bitcast_fusion.2
  599.7 2.0 dynamic-slice_bitcast_fusion.2
  741.9 47.8 %all-reduce = f32[2,8,384]{2,0,1:T(2,128)S(1)} all-reduce(f32[2,8,384]{2,0,1:T(2,128)S(1)} %copy.49), channel_id=2, replica_groups=mesh['tm'=64,'sta'=8] {'sta'}, use_global_device_ids=true, to_apply=%region_5.6.clone | all-reduce | flops 6144 | bytes 49152
  (510 shorter events, 273.4 us)
Async XLA Ops:
  0.0 279.4 %copy-start.4 = (s32[2,8,8]{2,1,0:T(8,128)S(1)}, s32[2,8,8]{2,1,0:T(8,128)}, u32[]{:S(2)}) copy-start(s32[2,8,8]{2,1,0:T(8,128)} %param.7) | copy-start | bytes 1540
  0.7 283.4 %collective-permute-start = (bf16[8,3,213]{2,0,1:T(8,128)(2,1)S(1)}, bf16[8,3,213]{2,0,1:T(8,128)(2,1)S(1)}, u32[]{:S(2)}, u32[]{:S(2)}) collective-permute-start(bf16[8,3,213]{2,0,1:T(8,128)(2,1)S(1)} %slice.9), channel_id=1, source_target_pairs={{8,0},{16,8},{24,16},{32,24},{40,32},{48,40},{56,48},{64,56},{72,6... | collective-permute-start | bytes 30680 | tf_op jit(solution)/shard_map/ppermute | solution.py:15
  296.6 98.9 %copy-start = (f32[8,448]{0,1:T(8,128)S(1)}, f32[8,448]{0,1:T(8,128)}, u32[]{:S(2)}) copy-start(f32[8,448]{0,1:T(8,128)} %copy.46) | copy-start | bytes 43012
  296.6 98.9 %copy-start.3 = (f32[8,16]{1,0:T(8,128)S(1)}, f32[8,16]{1,0:T(8,128)}, u32[]{:S(2)}) copy-start(f32[8,16]{1,0:T(8,128)} %copy.51) | copy-start | bytes 1540
  396.1 0.9 copy-start.1
  396.1 0.9 copy-start.2
where the time goes:
time: 804 us; the launch traced here: 791 us
  local copies, waits for them, and re-layouts  355 us (44%)
  blocking collectives  313 us (39%)
  matrix products  98.9 us (12%)
  other arithmetic  10.8 us (1%)
  starting transfers between devices  8.73 us (1%)
    gather x512, local copies, waits for them, and re-layouts  342 us
    psum x1, blocking collectives, shards(): batches = lax.psum(masked, 'tm').astype(jnp.bfloat16)  265 us
    conv_general_dilated x1, matrix products, correlate(): lax.conv_general_dilated(records, kernels, (1,), 'VALID', dimension_numbe...  98.9 us
    unnamed x1, blocking collectives  47.8 us
  transfers between devices with their start and end apart: 1, of which 0 were waited for; matrix products, arithmetic and copies ran while one was open for 1% of the time, Pallas kernels for 0%

commit v1 on v0

v1 whole, which is shorter than its diff:
```python
import jax
import jax.numpy as jnp
from jax import lax
from jax.experimental import pallas as pl
from jax.experimental.pallas import tpu as pltpu
from jax.sharding import PartitionSpec as P


MAXM = 64
STEP = 40
LANES = 128
WIN = 640

eps = 1e-06

VMEM = pl.BlockSpec(memory_space=pltpu.VMEM)
HBM = pl.BlockSpec(memory_space=pltpu.HBM)
LIMIT = pltpu.CompilerParams(vmem_limit_bytes=16 * 1024 * 1024)


def passed_along(block, axis, distance):
    devices = range(lax.axis_size(axis))
    route = [(i - distance, i) for i in devices if i - distance in devices]
    return lax.ppermute(block, axis, route)


def roll_left(value, amount):
    return pltpu.roll(value, value.shape[1] - amount, 1)


def pack_kernel(bank_hbm, data_hbm, owners_hbm, lags_hbm, out_ref, data_ref, owners_ref, lags_ref, bank_ref, given_ref, sems):
    moves = [
        pltpu.make_async_copy(bank_hbm, bank_ref, sems.at[0]),
        pltpu.make_async_copy(data_hbm, data_ref, sems.at[1]),
        pltpu.make_async_copy(owners_hbm, given_ref, sems.at[2]),
        pltpu.make_async_copy(lags_hbm, lags_ref, sems.at[3]),
    ]
    for move in moves:
        move.start()
    tmpl_count, comp_count, local_sta, span_len = bank_ref.shape
    groups = -(-span_len // STEP)
    rows = tmpl_count * local_sta
    lag = lax.broadcasted_iota(jnp.int32, (span_len, 1), 0)
    target = (lag // STEP) * LANES + lag % STEP
    lane = lax.broadcasted_iota(jnp.int32, (span_len, groups * LANES), 1)
    places = [
        jnp.where(lane == target + comp * STEP, 1.0, 0.0).astype(jnp.bfloat16) for comp in range(comp_count)
    ]
    to_row = lax.broadcasted_iota(jnp.int32, (rows * groups, 1), 0)
    source = ((to_row // groups) % tmpl_count) * local_sta + to_row // (groups * tmpl_count)
    from_row = lax.broadcasted_iota(jnp.int32, (rows * groups, rows), 1)
    reorders = [
        jnp.where(from_row == jnp.where(to_row % groups == group, source, -1), 1.0, 0.0).astype(jnp.bfloat16)
        for group in range(groups)
    ]
    moves[0].wait()
    packed = jnp.zeros((rows, groups * LANES), jnp.float32)
    for comp in range(comp_count):
        taps = bank_ref[:, comp].astype(jnp.float32).reshape(rows, span_len).astype(jnp.bfloat16)
        packed += jnp.dot(taps, places[comp], preferred_element_type=jnp.float32)
    packed = packed.astype(jnp.bfloat16)
    ordered = jnp.zeros((rows * groups, LANES), jnp.float32)
    for group in range(groups):
        piece = packed[:, group * LANES : (group + 1) * LANES]
        ordered += jnp.dot(reorders[group], piece, preferred_element_type=jnp.float32)
    out_ref[...] = ordered.astype(jnp.bfloat16)
    moves[2].wait()
    for b in range(owners_ref.shape[0]):
        owners_ref[b] = jnp.broadcast_to(given_ref[:, b : b + 1], owners_ref.shape[1:])
    moves[1].wait()
    moves[3].wait()


def pack(bank, data, owners, lags):
    tmpl_count, _, local_sta, span_len = bank.shape
    rows = local_sta * tmpl_count * -(-span_len // STEP)
    return pl.pallas_call(
        pack_kernel,
        out_shape=(
            jax.ShapeDtypeStruct((rows, LANES), jnp.bfloat16),
            jax.ShapeDtypeStruct(data.shape, data.dtype),
            jax.ShapeDtypeStruct((owners.shape[1], 8, LANES), jnp.int32),
            jax.ShapeDtypeStruct(lags.shape, lags.dtype),
        ),
        in_specs=[HBM] * 4,
        out_specs=(VMEM,) * 4,
        scratch_shapes=[
            pltpu.VMEM(bank.shape, bank.dtype),
            pltpu.VMEM(owners.shape, owners.dtype),
            pltpu.SemaphoreType.DMA((4,)),
        ],
        compiler_params=LIMIT,
        name="pack",
        cost_estimate=pl.CostEstimate(flops=40_000_000, bytes_accessed=200_000, transcendentals=0),
    )(*(pltpu.with_memory_space_constraint(x, pltpu.HBM) for x in (bank, data, owners, lags)))


def pick_kernel(owners_ref, seen_ref, out_ref):
    seen = seen_ref[...].astype(jnp.float32)
    _, groups, _ = seen.shape
    block = lax.broadcasted_iota(jnp.int32, seen.shape, 0)
    rows = []
    for b in range(owners_ref.shape[0]):
        chosen = block == owners_ref[b, :groups, :][None]
        rows.append(jnp.sum(jnp.where(chosen, seen, 0.0), axis=0))
    chunk = jnp.concatenate(rows, axis=0).astype(out_ref.dtype)
    out_ref[...] = jnp.broadcast_to(chunk[None], out_ref.shape)


def pick(owners, seen):
    blocks, groups, lanes = seen.shape
    return pl.pallas_call(
        pick_kernel,
        out_shape=jax.ShapeDtypeStruct((blocks, owners.shape[0] * groups, lanes), seen.dtype),
        in_specs=[VMEM, VMEM],
        out_specs=VMEM,
        compiler_params=LIMIT,
        name="pick",
        cost_estimate=pl.CostEstimate(flops=100_000, bytes_accessed=200_000, transcendentals=0),
    )(owners, seen)


def records_kernel(span_len, data_ref, edge_ref, hankel_ref, scale_ref):
    comp_count, local_sta, stretch_len = data_ref.shape
    row = lax.broadcasted_iota(jnp.int32, (8, WIN), 0)
    squares = jnp.zeros((local_sta, WIN), jnp.float32)
    windows = []
    for comp in range(comp_count):
        edge = edge_ref[comp, :, : WIN - stretch_len]
        record = jnp.concatenate([data_ref[comp].astype(jnp.float32), edge.astype(jnp.float32)], axis=1)
        squares += record * record
        windows.append(record)
    for sta in range(local_sta):
        parts = []
        for comp in range(comp_count):
            base = jnp.broadcast_to(windows[comp][sta : sta + 1], (8, WIN))
            for bit in (1, 2, 4):
                base = jnp.where((row & bit) != 0, roll_left(base, bit), base)
            parts += [base if lag == 0 else roll_left(base, lag) for lag in range(0, STEP, 8)]
        while len(parts) * 8 < LANES:
            parts.append(jnp.zeros((8, WIN), jnp.float32))
        for at in range(0, len(parts), 2):
            pair = jnp.concatenate(parts[at : at + 2], axis=0)
            hankel_ref[sta, at * 8 : at * 8 + 16, :] = pair.astype(jnp.bfloat16)
    run, total, at, width = squares, None, 0, 1
    while width <= span_len:
        if span_len & width:
            piece = run if at == 0 else roll_left(run, at)
            total = piece if total is None else total + piece
            at += width
        if 2 * width <= span_len:
            run = run + roll_left(run, width)
        width *= 2
    scale_ref[...] = 1.0 / jnp.sqrt(total / (comp_count * span_len) + eps)


def records(data, edge, span_len):
    _, local_sta, _ = data.shape
    return pl.pallas_call(
        lambda *refs: records_kernel(span_len, *refs),
        out_shape=(
            jax.ShapeDtypeStruct((local_sta, LANES, WIN), jnp.bfloat16),
            jax.ShapeDtypeStruct((local_sta, WIN), jnp.float32),
        ),
        in_specs=[VMEM, VMEM],
        out_specs=(VMEM, VMEM),
        compiler_params=LIMIT,
        name="records",
        cost_estimate=pl.CostEstimate(flops=8_000_000, bytes_accessed=4_000_000, transcendentals=4096),
    )(data, edge)


def stack_kernel(taps_count, tmpl_ref, hankel_ref, scale_ref, lag_ref, out_ref, wide_ref):
    tmpl_count, batch_count, stretch_len = out_ref.shape
    local_sta = hankel_ref.shape[0]
    groups = tmpl_ref.shape[1] // batch_count
    inner = batch_count * groups
    wide_ref[...] = tmpl_ref[...].astype(jnp.float32).reshape(wide_ref.shape)
    total = None
    for sta in range(local_sta):
        taps = []
        for group in range(groups):
            for batch in range(batch_count):
                start = sta * tmpl_count * inner + batch * groups + group
                taps.append(wide_ref[pl.ds(start, tmpl_count, stride=inner), :])
        left = jnp.concatenate(taps, axis=0)
        rows = batch_count * tmpl_count
        power = sum(left[g * rows : (g + 1) * rows] * left[g * rows : (g + 1) * rows] for g in range(groups))
        power = jnp.sum(power, axis=1, keepdims=True) / taps_count
        prods = jnp.dot(left.astype(jnp.bfloat16), hankel_ref[sta], preferred_element_type=jnp.float32)
        prod = prods[(groups - 1) * rows :]
        for group in range(groups - 2, -1, -1):
            prod = roll_left(prod, STEP) + prods[group * rows : (group + 1) * rows]
        scores = prod * (1.0 / (taps_count * jnp.sqrt(power + eps))) * scale_ref[sta : sta + 1, :]
        scores = scores[:, : stretch_len + 128]
        lags = lag_ref[:, sta : sta + 1]
        bit = 1
        while bit <= MAXM:
            scores = jnp.where((lags & bit) != 0, roll_left(scores, bit), scores)
            bit *= 2
        total = scores if total is None else total + scores
    for batch in range(batch_count):
        out_ref[:, batch, :] = total[batch * tmpl_count : (batch + 1) * tmpl_count, :stretch_len]


def stack(tmpl, hankel, scale, lags, taps_count, out_shape):
    return pl.pallas_call(
        lambda *refs: stack_kernel(taps_count, *refs),
        out_shape=jax.ShapeDtypeStruct(out_shape, jnp.float32),
        in_specs=[VMEM] * 4,
        out_specs=VMEM,
        scratch_shapes=[pltpu.VMEM((tmpl.shape[0] * tmpl.shape[1], LANES), jnp.float32)],
        compiler_params=LIMIT,
        name="stack",
        cost_estimate=pl.CostEstimate(flops=60_000_000, bytes_accessed=4_000_000, transcendentals=4096),
    )(tmpl, hankel, scale, lags)


def shards(data, bank, owners, moveouts):
    local_sta, comp_count, stretch_len = data.shape
    span_len = bank.shape[-1]
    tmpl_count = bank.shape[1]
    batch_count = owners.shape[0]
    blocks = lax.axis_size("tm")
    source = jnp.transpose(data, (1, 0, 2))
    lags = moveouts.reshape(batch_count * tmpl_count, local_sta)
    slot, series, owned, lags = pack(jnp.transpose(bank[0], (0, 2, 1, 3)), source, owners[None], lags)
    seen = lax.all_to_all(slot.reshape(blocks, -1, LANES), "tm", 0, 0, tiled=True)
    edge = passed_along(source, "tm", -1)
    chosen = pick(owned, seen)
    tmpl = lax.all_to_all(chosen, "tm", 0, 0, tiled=True)
    hankel, scale = records(series, edge, span_len)
    partial_sum = stack(
        tmpl, hankel, scale, lags, comp_count * span_len, (tmpl_count, batch_count, stretch_len)
    )
    pieces = lax.all_to_all(partial_sum, "sta", 0, 0, tiled=True)
    return jnp.sum(pieces, axis=0)[:, None, :]


def solution(mesh):
    placed = (P("sta", None, "tm"), P("tm", None, "sta", None, None), P(), P(None, None, "sta"))
    return jax.shard_map(
        shards, mesh=mesh, in_specs=placed, out_specs=P(None, "sta", "tm"), check_vma=False
    )
```

time: 804 us -> 63.5 us (0.08); the launches traced: 791 us -> 63.2 us
  local copies, waits for them, and re-layouts: 355 us -> 0.58 us
  blocking collectives: 313 us -> 43.2 us
  matrix products: 98.9 us -> 0 us
  other arithmetic: 10.8 us -> 0.02 us
    gather x513 -> x0, local copies, waits for them, and re-layouts: 343 us -> none
    psum x1 -> x0, blocking collectives: 265 us -> none  [shards(): batches = lax.psum(masked, 'tm').astype(jnp.bfloat16)]
    conv_general_dilated x1 -> x0, matrix products: 98.9 us -> none  [correlate(): lax.conv_general_dilated(records, kernels, (1,), 'VALID', dimension_numbe...]
    unnamed x1 -> x0, blocking collectives: 47.8 us -> none
    all_to_all x0 -> x2, blocking collectives: none -> 43.2 us  [the longest x1 24.5 us: shards(): lax.all_to_all(slot.reshape(blocks, -1, LANES), 'tm', 0, 0, tiled=True)]
    another operation x2 -> x0, other arithmetic: 9.14 us -> none  [the longest x1 9.11 us: correlate(): lax.reduce_window(squares, 0.0, lax.add, (1, span_len), (1, 1), 'VALID')]
  transfers between devices with their start and end apart: 1 -> 2, of which waited for: 0 -> 2; matrix products, arithmetic and copies ran while one was open for 1% -> 0% of each run, Pallas kernels for 0% -> 5%
where the time goes in v1:
time: 63.5 us; the launch traced here: 63.2 us
  blocking collectives  43.2 us (68%)
  Pallas kernels  7.25 us (11%)
  starting transfers between devices  6.91 us (11%)
  waiting for transfers between devices  5.23 us (8%)
    all_to_all x1, blocking collectives, shards(): lax.all_to_all(slot.reshape(blocks, -1, LANES), 'tm', 0, 0, tiled=True)  24.5 us
    all_to_all x1, blocking collectives, shards(): pieces = lax.all_to_all(partial_sum, 'sta', 0, 0, tiled=True)  18.6 us
    all_to_all x1, starting transfers between devices, shards(): tmpl = lax.all_to_all(chosen, 'tm', 0, 0, tiled=True)  4.43 us
    ppermute x1, waiting for transfers between devices, passed_along(): return lax.ppermute(block, axis, route)  3.34 us
    pallas_call x1, Pallas kernels, records(): pl.pallas_call(lambda *refs: records_kernel(span_len, *refs), out_shape=(...  3.33 us
    ppermute x1, starting transfers between devices, passed_along(): return lax.ppermute(block, axis, route)  2.48 us
    all_to_all x1, waiting for transfers between devices, shards(): tmpl = lax.all_to_all(chosen, 'tm', 0, 0, tiled=True)  1.89 us
    pallas_call x1, Pallas kernels, stack(): pl.pallas_call(lambda *refs: stack_kernel(taps_count, *refs), out_shape=j...  1.76 us
  transfers between devices with their start and end apart: 2, of which 2 were waited for; matrix products, arithmetic and copies ran while one was open for 0% of the time, Pallas kernels for 5%

profile of v1, /device:TPU:1, one launch (start us, length us, event | category | flops | bytes accessed | tf_op | source)
XLA Modules:
  0.0 63.2 jit_solution(16326766567274222946)
XLA Ops:
  0.0 1.4 %pack.1 = (bf16[256,128]{1,0:T(8,128)(2,1)S(1)}, bf16[3,8,384]{2,1,0:T(8,128)(2,1)S(1)}, s32[2,8,128]{2,1,0:T(8,128)S(1)}, s32[16,8]{1,0:T(8,128)S(1)}) custom-call(bf16[8,3,8,150]{3,2,1,0:T(8,128)(2,1)} %bitcast.8, bf16[3,8,384]{2,1,0:T(8,128)(2,1)} %bitcast.9, s32[1,2]{1,0:T(1,128)} %bitcast.12, s32[16,8]{1,0:T(8,128)} %bitcast.11), custom_call_target="tpu_custom_call" | custom-call | flops 40000000 | bytes 200000 | tf_op jit(solution)/shard_map/pack/pallas_call | solution.py:77
  1.4 24.5 %all_to_all.15.seen_ref = bf16[64,4,128]{2,1,0:T(4,128)(2,1)S(1)} all-to-all(bf16[64,4,128]{2,1,0:T(4,128)(2,1)S(1)} %bitcast.7), channel_id=1, replica_groups=mesh['tm'=64,'sta'=8] {'tm'}, dimensions={0} | all-to-all | bytes 131072 | tf_op jit(solution)/shard_map/all_to_all | solution.py:228
  25.9 0.8 %pick.1 = bf16[64,8,128]{2,1,0:T(8,128)(2,1)} custom-call(s32[2,8,128]{2,1,0:T(8,128)S(1)} %get-tuple-element.11.owners_ref, bf16[64,4,128]{2,1,0:T(4,128)(2,1)S(1)} %all_to_all.15.seen_ref), custom_call_target="tpu_custom_call" | custom-call | flops 100000 | bytes 200000 | tf_op jit(solution)/shard_map/pick/pallas_call | solution.py:112
  26.7 4.4 %all-to-all-start.1 = ((bf16[64,8,128]{2,1,0:T(8,128)(2,1)}), bf16[64,8,128]{2,1,0:T(8,128)(2,1)S(1)}, u32[]{:S(2)}, u32[]{:S(2)}) async-start(bf16[64,8,128]{2,1,0:T(8,128)(2,1)} %pick.1), calls=%async_computation.1 | async-start | bytes 262144 | tf_op jit(solution)/shard_map/all_to_all | solution.py:231
  31.1 2.5 %collective-permute-start = (bf16[3,8,384]{2,1,0:T(8,128)(2,1)}, bf16[3,8,384]{2,1,0:T(8,128)(2,1)S(1)}, u32[]{:S(2)}, u32[]{:S(2)}) collective-permute-start(bf16[3,8,384]{2,1,0:T(8,128)(2,1)} %bitcast.10), channel_id=1, source_target_pairs={{8,0},{16,8},{24,16},{32,24},{40,32},{48,40},{56,48},{64,56},{72,6... | collective-permute-start | bytes 55304 | tf_op jit(solution)/shard_map/ppermute | solution.py:24
  33.6 3.3 %collective-permute-done.refs_1_ = bf16[3,8,384]{2,1,0:T(8,128)(2,1)S(1)} collective-permute-done((bf16[3,8,384]{2,1,0:T(8,128)(2,1)}, bf16[3,8,384]{2,1,0:T(8,128)(2,1)S(1)}, u32[]{:S(2)}, u32[]{:S(2)}) %collective-permute-start) | collective-permute-done | bytes 18464 | tf_op jit(solution)/shard_map/ppermute | solution.py:24
  36.9 3.3 %records.1 = (bf16[8,128,640]{2,1,0:T(8,128)(2,1)S(1)}, f32[8,640]{1,0:T(8,128)S(1)}) custom-call(bf16[3,8,384]{2,1,0:T(8,128)(2,1)S(1)} %get-tuple-element.13.refs_0_, bf16[3,8,384]{2,1,0:T(8,128)(2,1)S(1)} %collective-permute-done.refs_1_), custom_call_target="tpu_custom_call" | custom-call | flops 8000000 | bytes 4000000 | tf_op jit(solution)/shard_map/records/pallas_call | solution.py:159
  40.3 1.9 %all-to-all-done.1.refs_0_ = bf16[64,8,128]{2,1,0:T(8,128)(2,1)S(1)} async-done(((bf16[64,8,128]{2,1,0:T(8,128)(2,1)}), bf16[64,8,128]{2,1,0:T(8,128)(2,1)S(1)}, u32[]{:S(2)}, u32[]{:S(2)}) %all-to-all-start.1) | async-done | bytes 131104 | tf_op jit(solution)/shard_map/all_to_all | solution.py:231
  42.2 1.8 %stack.1 = f32[8,2,384]{2,1,0:T(2,128)S(1)} custom-call(bf16[64,8,128]{2,1,0:T(8,128)(2,1)S(1)} %all-to-all-done.1.refs_0_, bf16[8,128,640]{2,1,0:T(8,128)(2,1)S(1)} %get-tuple-element.14.refs_1_, f32[8,640]{1,0:T(8,128)S(1)} %get-tuple-element.15.refs_2_, s32[16,8]{1,0:T(8,128)S(1)} %get-tuple-element.16.refs_3_), custom_call_target="tpu_custom_call" | custom-call | flops 60000000 | bytes 4000000 | tf_op jit(solution)/shard_map/stack/pallas_call | solution.py:207
  43.9 18.6 %all_to_all.16 = f32[8,2,384]{2,1,0:T(2,128)S(1)} all-to-all(f32[8,2,384]{2,1,0:T(2,128)S(1)} %stack.1), channel_id=1, replica_groups=mesh['tm'=64,'sta'=8] {'sta'}, dimensions={0} | all-to-all | bytes 49152 | tf_op jit(solution)/shard_map/all_to_all | solution.py:236
  62.6 0.6 broadcast_in_dim.7
  (1 shorter events, 0.0 us)
Async XLA Ops:
  26.7 15.5 %all-to-all-start.1 = ((bf16[64,8,128]{2,1,0:T(8,128)(2,1)}), bf16[64,8,128]{2,1,0:T(8,128)(2,1)S(1)}, u32[]{:S(2)}, u32[]{:S(2)}) async-start(bf16[64,8,128]{2,1,0:T(8,128)(2,1)} %pick.1), calls=%async_computation.1 | async-start | bytes 262144 | tf_op jit(solution)/shard_map/all_to_all | solution.py:231
  31.1 5.8 %collective-permute-start = (bf16[3,8,384]{2,1,0:T(8,128)(2,1)}, bf16[3,8,384]{2,1,0:T(8,128)(2,1)S(1)}, u32[]{:S(2)}, u32[]{:S(2)}) collective-permute-start(bf16[3,8,384]{2,1,0:T(8,128)(2,1)} %bitcast.10), channel_id=1, source_target_pairs={{8,0},{16,8},{24,16},{32,24},{40,32},{48,40},{56,48},{64,56},{72,6... | collective-permute-start | bytes 55304 | tf_op jit(solution)/shard_map/ppermute | solution.py:24

commit v2 on v1

--- a/solution.py
+++ b/solution.py
@@ -6,7 +6,6 @@
 from jax.sharding import PartitionSpec as P
 
 
-MAXM = 64
 STEP = 40
 LANES = 128
 WIN = 640
@@ -28,7 +27,11 @@
     return pltpu.roll(value, value.shape[1] - amount, 1)
 
 
-def pack_kernel(bank_hbm, data_hbm, owners_hbm, lags_hbm, out_ref, data_ref, owners_ref, lags_ref, bank_ref, given_ref, sems):
+def turn(value, source):
+    return jnp.take_along_axis(value, source & 127, axis=1, mode="promise_in_bounds")
+
+
+def pack_kernel(bank_hbm, data_hbm, owners_hbm, lags_hbm, out_ref, data_ref, owners_ref, lags_ref, bank_ref, given_ref, wide_ref, sems):
     moves = [
         pltpu.make_async_copy(bank_hbm, bank_ref, sems.at[0]),
         pltpu.make_async_copy(data_hbm, data_ref, sems.at[1]),
@@ -38,7 +41,7 @@
     for move in moves:
         move.start()
     tmpl_count, comp_count, local_sta, span_len = bank_ref.shape
-    groups = -(-span_len // STEP)
+    groups = out_ref.shape[0] // (tmpl_count * local_sta)
     rows = tmpl_count * local_sta
     lag = lax.broadcasted_iota(jnp.int32, (span_len, 1), 0)
     target = (lag // STEP) * LANES + lag % STEP
@@ -46,24 +49,15 @@
     places = [
         jnp.where(lane == target + comp * STEP, 1.0, 0.0).astype(jnp.bfloat16) for comp in range(comp_count)
     ]
-    to_row = lax.broadcasted_iota(jnp.int32, (rows * groups, 1), 0)
-    source = ((to_row // groups) % tmpl_count) * local_sta + to_row // (groups * tmpl_count)
-    from_row = lax.broadcasted_iota(jnp.int32, (rows * groups, rows), 1)
-    reorders = [
-        jnp.where(from_row == jnp.where(to_row % groups == group, source, -1), 1.0, 0.0).astype(jnp.bfloat16)
-        for group in range(groups)
-    ]
     moves[0].wait()
-    packed = jnp.zeros((rows, groups * LANES), jnp.float32)
+    packed = None
     for comp in range(comp_count):
         taps = bank_ref[:, comp].astype(jnp.float32).reshape(rows, span_len).astype(jnp.bfloat16)
-        packed += jnp.dot(taps, places[comp], preferred_element_type=jnp.float32)
-    packed = packed.astype(jnp.bfloat16)
-    ordered = jnp.zeros((rows * groups, LANES), jnp.float32)
+        placed = jnp.dot(taps, places[comp], preferred_element_type=jnp.float32)
+        packed = placed if packed is None else packed + placed
     for group in range(groups):
-        piece = packed[:, group * LANES : (group + 1) * LANES]
-        ordered += jnp.dot(reorders[group], piece, preferred_element_type=jnp.float32)
-    out_ref[...] = ordered.astype(jnp.bfloat16)
+        wide_ref[pl.ds(group, rows, stride=groups), :] = packed[:, group * LANES : (group + 1) * LANES]
+    out_ref[...] = wide_ref[...].astype(jnp.bfloat16)
     moves[2].wait()
     for b in range(owners_ref.shape[0]):
         owners_ref[b] = jnp.broadcast_to(given_ref[:, b : b + 1], owners_ref.shape[1:])
@@ -87,6 +81,7 @@
         scratch_shapes=[
             pltpu.VMEM(bank.shape, bank.dtype),
             pltpu.VMEM(owners.shape, owners.dtype),
+            pltpu.VMEM((rows, LANES), jnp.float32),
             pltpu.SemaphoreType.DMA((4,)),
         ],
         compiler_params=LIMIT,
@@ -122,7 +117,7 @@
 
 def records_kernel(span_len, data_ref, edge_ref, hankel_ref, scale_ref):
     comp_count, local_sta, stretch_len = data_ref.shape
-    row = lax.broadcasted_iota(jnp.int32, (8, WIN), 0)
+    tiles = WIN // 128
     squares = jnp.zeros((local_sta, WIN), jnp.float32)
     windows = []
     for comp in range(comp_count):
@@ -130,18 +125,21 @@
         record = jnp.concatenate([data_ref[comp].astype(jnp.float32), edge.astype(jnp.float32)], axis=1)
         squares += record * record
         windows.append(record)
+    row = lax.broadcasted_iota(jnp.int32, (STEP, 128), 0)
+    lane = lax.broadcasted_iota(jnp.int32, (STEP, 128), 1)
+    spare = jnp.zeros((LANES - comp_count * STEP, 128), jnp.float32)
     for sta in range(local_sta):
-        parts = []
+        turned = []
         for comp in range(comp_count):
-            base = jnp.broadcast_to(windows[comp][sta : sta + 1], (8, WIN))
-            for bit in (1, 2, 4):
-                base = jnp.where((row & bit) != 0, roll_left(base, bit), base)
-            parts += [base if lag == 0 else roll_left(base, lag) for lag in range(0, STEP, 8)]
-        while len(parts) * 8 < LANES:
-            parts.append(jnp.zeros((8, WIN), jnp.float32))
-        for at in range(0, len(parts), 2):
-            pair = jnp.concatenate(parts[at : at + 2], axis=0)
-            hankel_ref[sta, at * 8 : at * 8 + 16, :] = pair.astype(jnp.bfloat16)
+            parts = []
+            for tile in range(tiles):
+                base = windows[comp][sta : sta + 1, tile * 128 : (tile + 1) * 128]
+                parts.append(turn(jnp.broadcast_to(base, (STEP, 128)), lane + row))
+            turned.append(parts)
+        for tile in range(tiles):
+            after = (tile + 1) % tiles
+            block = [jnp.where(lane + row < 128, parts[tile], parts[after]) for parts in turned]
+            hankel_ref[sta, :, tile * 128 : (tile + 1) * 128] = jnp.concatenate(block + [spare], axis=0).astype(jnp.bfloat16)
     run, total, at, width = squares, None, 0, 1
     while width <= span_len:
         if span_len & width:
@@ -175,32 +173,32 @@
     local_sta = hankel_ref.shape[0]
     groups = tmpl_ref.shape[1] // batch_count
     inner = batch_count * groups
+    tiles = stretch_len // 128
+    lane = lax.broadcasted_iota(jnp.int32, (batch_count * tmpl_count, 128), 1)
     wide_ref[...] = tmpl_ref[...].astype(jnp.float32).reshape(wide_ref.shape)
     total = None
     for sta in range(local_sta):
         taps = []
         for group in range(groups):
             for batch in range(batch_count):
-                start = sta * tmpl_count * inner + batch * groups + group
-                taps.append(wide_ref[pl.ds(start, tmpl_count, stride=inner), :])
+                start = sta * inner + batch * groups + group
+                taps.append(wide_ref[pl.ds(start, tmpl_count, stride=local_sta * inner), :])
         left = jnp.concatenate(taps, axis=0)
         rows = batch_count * tmpl_count
         power = sum(left[g * rows : (g + 1) * rows] * left[g * rows : (g + 1) * rows] for g in range(groups))
         power = jnp.sum(power, axis=1, keepdims=True) / taps_count
         prods = jnp.dot(left.astype(jnp.bfloat16), hankel_ref[sta], preferred_element_type=jnp.float32)
-        prod = prods[(groups - 1) * rows :]
-        for group in range(groups - 2, -1, -1):
-            prod = roll_left(prod, STEP) + prods[group * rows : (group + 1) * rows]
+        prod = prods[:rows]
+        for group in range(1, groups):
+            prod += roll_left(prods[group * rows : (group + 1) * rows], group * STEP)
         scores = prod * (1.0 / (taps_count * jnp.sqrt(power + eps))) * scale_ref[sta : sta + 1, :]
-        scores = scores[:, : stretch_len + 128]
-        lags = lag_ref[:, sta : sta + 1]
-        bit = 1
-        while bit <= MAXM:
-            scores = jnp.where((lags & bit) != 0, roll_left(scores, bit), scores)
-            bit *= 2
-        total = scores if total is None else total + scores
+        source = lane + lag_ref[:, sta : sta + 1]
+        turned = [turn(scores[:, t * 128 : (t + 1) * 128], source) for t in range(tiles + 1)]
+        shifted = [jnp.where(source < 128, turned[t], turned[t + 1]) for t in range(tiles)]
+        total = shifted if total is None else [x + y for x, y in zip(total, shifted)]
+    total = jnp.concatenate(total, axis=1)
     for batch in range(batch_count):
-        out_ref[:, batch, :] = total[batch * tmpl_count : (batch + 1) * tmpl_count, :stretch_len]
+        out_ref[:, batch, :] = total[batch * tmpl_count : (batch + 1) * tmpl_count]
 
 
 def stack(tmpl, hankel, scale, lags, taps_count, out_shape):

time: 63.5 us -> 62.5 us (0.984)
  Pallas kernels: 7.25 us -> 4.34 us
  waiting for transfers between devices: 5.23 us -> 7.2 us
    all_to_all x1, waiting for transfers between devices: 1.89 us -> 3.86 us  [shards(): tmpl = lax.all_to_all(chosen, 'tm', 0, 0, tiled=True)]
    pallas_call x1, Pallas kernels: 3.33 us -> 1.36 us  [records(): pl.pallas_call(lambda *refs: records_kernel(span_len, *refs), out_shape=(...]
    pallas_call x1, Pallas kernels: 1.76 us -> 1.01 us  [stack(): pl.pallas_call(lambda *refs: stack_kernel(taps_count, *refs), out_shape=j...]
  transfers between devices with their start and end apart: 2 -> 2, of which waited for: 2 -> 2; matrix products, arithmetic and copies ran while one was open for 0% -> 0% of each run, Pallas kernels for 5% -> 2%
where the time goes in v2:
time: 62.5 us; the launch traced here: 62.3 us
  blocking collectives  43.2 us (69%)
  waiting for transfers between devices  7.2 us (12%)
  starting transfers between devices  6.91 us (11%)
  Pallas kernels  4.34 us (7%)
    all_to_all x1, blocking collectives, shards(): lax.all_to_all(slot.reshape(blocks, -1, LANES), 'tm', 0, 0, tiled=True)  24.5 us
    all_to_all x1, blocking collectives, shards(): pieces = lax.all_to_all(partial_sum, 'sta', 0, 0, tiled=True)  18.7 us
    all_to_all x1, starting transfers between devices, shards(): tmpl = lax.all_to_all(chosen, 'tm', 0, 0, tiled=True)  4.43 us
    all_to_all x1, waiting for transfers between devices, shards(): tmpl = lax.all_to_all(chosen, 'tm', 0, 0, tiled=True)  3.86 us
    ppermute x1, waiting for transfers between devices, passed_along(): return lax.ppermute(block, axis, route)  3.34 us
    ppermute x1, starting transfers between devices, passed_along(): return lax.ppermute(block, axis, route)  2.48 us
    pallas_call x1, Pallas kernels, records(): pl.pallas_call(lambda *refs: records_kernel(span_len, *refs), out_shape=(...  1.36 us
  transfers between devices with their start and end apart: 2, of which 2 were waited for; matrix products, arithmetic and copies ran while one was open for 0% of the time, Pallas kernels for 2%

profile of v2, /device:TPU:1, one launch (start us, length us, event | category | flops | bytes accessed | tf_op | source)
XLA Modules:
  0.0 62.3 jit_solution(6892195428180206790)
XLA Ops:
  0.0 1.2 %pack.1 = (bf16[256,128]{1,0:T(8,128)(2,1)S(1)}, bf16[3,8,384]{2,1,0:T(8,128)(2,1)S(1)}, s32[2,8,128]{2,1,0:T(8,128)S(1)}, s32[16,8]{1,0:T(8,128)S(1)}) custom-call(bf16[8,3,8,150]{3,2,1,0:T(8,128)(2,1)} %bitcast.8, bf16[3,8,384]{2,1,0:T(8,128)(2,1)} %bitcast.9, s32[1,2]{1,0:T(1,128)} %bitcast.12, s32[16,8]{1,0:T(8,128)} %bitcast.11), custom_call_target="tpu_custom_call" | custom-call | flops 40000000 | bytes 200000 | tf_op jit(solution)/shard_map/pack/pallas_call | solution.py:71
  1.2 24.5 %all_to_all.15.seen_ref = bf16[64,4,128]{2,1,0:T(4,128)(2,1)S(1)} all-to-all(bf16[64,4,128]{2,1,0:T(4,128)(2,1)S(1)} %bitcast.7), channel_id=1, replica_groups=mesh['tm'=64,'sta'=8] {'tm'}, dimensions={0} | all-to-all | bytes 131072 | tf_op jit(solution)/shard_map/all_to_all | solution.py:226
  25.7 0.8 %pick.1 = bf16[64,8,128]{2,1,0:T(8,128)(2,1)} custom-call(s32[2,8,128]{2,1,0:T(8,128)S(1)} %get-tuple-element.11.owners_ref, bf16[64,4,128]{2,1,0:T(4,128)(2,1)S(1)} %all_to_all.15.seen_ref), custom_call_target="tpu_custom_call" | custom-call | flops 100000 | bytes 200000 | tf_op jit(solution)/shard_map/pick/pallas_call | solution.py:107
  26.5 4.4 %all-to-all-start.1 = ((bf16[64,8,128]{2,1,0:T(8,128)(2,1)}), bf16[64,8,128]{2,1,0:T(8,128)(2,1)S(1)}, u32[]{:S(2)}, u32[]{:S(2)}) async-start(bf16[64,8,128]{2,1,0:T(8,128)(2,1)} %pick.1), calls=%async_computation.1 | async-start | bytes 262144 | tf_op jit(solution)/shard_map/all_to_all | solution.py:229
  30.9 2.5 %collective-permute-start = (bf16[3,8,384]{2,1,0:T(8,128)(2,1)}, bf16[3,8,384]{2,1,0:T(8,128)(2,1)S(1)}, u32[]{:S(2)}, u32[]{:S(2)}) collective-permute-start(bf16[3,8,384]{2,1,0:T(8,128)(2,1)} %bitcast.10), channel_id=1, source_target_pairs={{8,0},{16,8},{24,16},{32,24},{40,32},{48,40},{56,48},{64,56},{72,6... | collective-permute-start | bytes 55304 | tf_op jit(solution)/shard_map/ppermute | solution.py:23
  33.4 3.3 %collective-permute-done.refs_1_ = bf16[3,8,384]{2,1,0:T(8,128)(2,1)S(1)} collective-permute-done((bf16[3,8,384]{2,1,0:T(8,128)(2,1)}, bf16[3,8,384]{2,1,0:T(8,128)(2,1)S(1)}, u32[]{:S(2)}, u32[]{:S(2)}) %collective-permute-start) | collective-permute-done | bytes 18464 | tf_op jit(solution)/shard_map/ppermute | solution.py:23
  36.8 1.4 %records.1 = (bf16[8,128,640]{2,1,0:T(8,128)(2,1)S(1)}, f32[8,640]{1,0:T(8,128)S(1)}) custom-call(bf16[3,8,384]{2,1,0:T(8,128)(2,1)S(1)} %get-tuple-element.13.refs_0_, bf16[3,8,384]{2,1,0:T(8,128)(2,1)S(1)} %collective-permute-done.refs_1_), custom_call_target="tpu_custom_call" | custom-call | flops 8000000 | bytes 4000000 | tf_op jit(solution)/shard_map/records/pallas_call | solution.py:157
  38.1 3.9 %all-to-all-done.1.refs_0_ = bf16[64,8,128]{2,1,0:T(8,128)(2,1)S(1)} async-done(((bf16[64,8,128]{2,1,0:T(8,128)(2,1)}), bf16[64,8,128]{2,1,0:T(8,128)(2,1)S(1)}, u32[]{:S(2)}, u32[]{:S(2)}) %all-to-all-start.1) | async-done | bytes 131104 | tf_op jit(solution)/shard_map/all_to_all | solution.py:229
  42.0 1.0 %stack.1 = f32[8,2,384]{2,1,0:T(2,128)S(1)} custom-call(bf16[64,8,128]{2,1,0:T(8,128)(2,1)S(1)} %all-to-all-done.1.refs_0_, bf16[8,128,640]{2,1,0:T(8,128)(2,1)S(1)} %get-tuple-element.14.refs_1_, f32[8,640]{1,0:T(8,128)S(1)} %get-tuple-element.15.refs_2_, s32[16,8]{1,0:T(8,128)S(1)} %get-tuple-element.16.refs_3_), custom_call_target="tpu_custom_call" | custom-call | flops 60000000 | bytes 4000000 | tf_op jit(solution)/shard_map/stack/pallas_call | solution.py:205
  43.0 18.7 %all_to_all.16 = f32[8,2,384]{2,1,0:T(2,128)S(1)} all-to-all(f32[8,2,384]{2,1,0:T(2,128)S(1)} %stack.1), channel_id=1, replica_groups=mesh['tm'=64,'sta'=8] {'sta'}, dimensions={0} | all-to-all | bytes 49152 | tf_op jit(solution)/shard_map/all_to_all | solution.py:234
  61.7 0.6 broadcast_in_dim.7
  (1 shorter events, 0.0 us)
Async XLA Ops:
  26.5 15.5 %all-to-all-start.1 = ((bf16[64,8,128]{2,1,0:T(8,128)(2,1)}), bf16[64,8,128]{2,1,0:T(8,128)(2,1)S(1)}, u32[]{:S(2)}, u32[]{:S(2)}) async-start(bf16[64,8,128]{2,1,0:T(8,128)(2,1)} %pick.1), calls=%async_computation.1 | async-start | bytes 262144 | tf_op jit(solution)/shard_map/all_to_all | solution.py:229
  30.9 5.8 %collective-permute-start = (bf16[3,8,384]{2,1,0:T(8,128)(2,1)}, bf16[3,8,384]{2,1,0:T(8,128)(2,1)S(1)}, u32[]{:S(2)}, u32[]{:S(2)}) collective-permute-start(bf16[3,8,384]{2,1,0:T(8,128)(2,1)} %bitcast.10), channel_id=1, source_target_pairs={{8,0},{16,8},{24,16},{32,24},{40,32},{48,40},{56,48},{64,56},{72,6... | collective-permute-start | bytes 55304 | tf_op jit(solution)/shard_map/ppermute | solution.py:23

commit v3 on v2

--- a/solution.py
+++ b/solution.py
@@ -31,82 +31,102 @@
     return jnp.take_along_axis(value, source & 127, axis=1, mode="promise_in_bounds")
 
 
-def pack_kernel(bank_hbm, data_hbm, owners_hbm, lags_hbm, out_ref, data_ref, owners_ref, lags_ref, bank_ref, given_ref, wide_ref, sems):
+def load_kernel(data_hbm, owners_hbm, lags_hbm, data_ref, owners_ref, lags_ref, place_ref, given_ref, sems):
     moves = [
-        pltpu.make_async_copy(bank_hbm, bank_ref, sems.at[0]),
+        pltpu.make_async_copy(owners_hbm, given_ref, sems.at[0]),
         pltpu.make_async_copy(data_hbm, data_ref, sems.at[1]),
-        pltpu.make_async_copy(owners_hbm, given_ref, sems.at[2]),
-        pltpu.make_async_copy(lags_hbm, lags_ref, sems.at[3]),
+        pltpu.make_async_copy(lags_hbm, lags_ref, sems.at[2]),
     ]
     for move in moves:
         move.start()
-    tmpl_count, comp_count, local_sta, span_len = bank_ref.shape
-    groups = out_ref.shape[0] // (tmpl_count * local_sta)
-    rows = tmpl_count * local_sta
+    comp_count, span_len, width = place_ref.shape
     lag = lax.broadcasted_iota(jnp.int32, (span_len, 1), 0)
     target = (lag // STEP) * LANES + lag % STEP
-    lane = lax.broadcasted_iota(jnp.int32, (span_len, groups * LANES), 1)
-    places = [
-        jnp.where(lane == target + comp * STEP, 1.0, 0.0).astype(jnp.bfloat16) for comp in range(comp_count)
-    ]
+    lane = lax.broadcasted_iota(jnp.int32, (span_len, width), 1)
+    for comp in range(comp_count):
+        place_ref[comp] = jnp.where(lane == target + comp * STEP, 1.0, 0.0).astype(jnp.bfloat16)
     moves[0].wait()
+    for b in range(owners_ref.shape[0]):
+        owners_ref[b] = jnp.broadcast_to(given_ref[:, b : b + 1], owners_ref.shape[1:])
+    moves[1].wait()
+    moves[2].wait()
+
+
+def load(data, owners, lags, span_len):
+    given = [pltpu.with_memory_space_constraint(x, pltpu.HBM) for x in (data, owners, lags)]
+    width = -(-span_len // STEP) * LANES
+    return pl.pallas_call(
+        load_kernel,
+        out_shape=(
+            jax.ShapeDtypeStruct(data.shape, data.dtype),
+            jax.ShapeDtypeStruct((owners.shape[1], 8, LANES), jnp.int32),
+            jax.ShapeDtypeStruct(lags.shape, lags.dtype),
+            jax.ShapeDtypeStruct((data.shape[0], span_len, width), jnp.bfloat16),
+        ),
+        in_specs=[HBM] * 3,
+        out_specs=(VMEM,) * 4,
+        scratch_shapes=[pltpu.VMEM(owners.shape, owners.dtype), pltpu.SemaphoreType.DMA((3,))],
+        compiler_params=LIMIT,
+        name="load",
+        cost_estimate=pl.CostEstimate(flops=500_000, bytes_accessed=500_000, transcendentals=0),
+    )(*given)
+
+
+def chosen_source(seen, source):
+    block = lax.broadcasted_iota(jnp.int32, seen.shape, 0)
+    return jnp.sum(jnp.where(block == source, seen, 0.0), axis=0)
+
+
+def repack_kernel(owners_ref, seen_ref, place_ref, out_ref, wide_ref):
+    peers, comp_count, local_sta, _ = seen_ref.shape
+    batch_count = owners_ref.shape[0]
+    groups = place_ref.shape[2] // LANES
+    rows = batch_count * local_sta
     packed = None
     for comp in range(comp_count):
-        taps = bank_ref[:, comp].astype(jnp.float32).reshape(rows, span_len).astype(jnp.bfloat16)
-        placed = jnp.dot(taps, places[comp], preferred_element_type=jnp.float32)
+        taps = []
+        for b in range(batch_count):
+            owner = owners_ref[b, 0:1, 0:1] % peers
+            taps.append(chosen_source(seen_ref[:, comp].astype(jnp.float32), owner[None]))
+        taps = jnp.concatenate(taps, axis=0).astype(jnp.bfloat16)
+        placed = jnp.dot(taps, place_ref[comp], preferred_element_type=jnp.float32)
         packed = placed if packed is None else packed + placed
     for group in range(groups):
         wide_ref[pl.ds(group, rows, stride=groups), :] = packed[:, group * LANES : (group + 1) * LANES]
-    out_ref[...] = wide_ref[...].astype(jnp.bfloat16)
-    moves[2].wait()
-    for b in range(owners_ref.shape[0]):
-        owners_ref[b] = jnp.broadcast_to(given_ref[:, b : b + 1], owners_ref.shape[1:])
-    moves[1].wait()
-    moves[3].wait()
-
-
-def pack(bank, data, owners, lags):
-    tmpl_count, _, local_sta, span_len = bank.shape
-    rows = local_sta * tmpl_count * -(-span_len // STEP)
-    return pl.pallas_call(
-        pack_kernel,
-        out_shape=(
-            jax.ShapeDtypeStruct((rows, LANES), jnp.bfloat16),
-            jax.ShapeDtypeStruct(data.shape, data.dtype),
-            jax.ShapeDtypeStruct((owners.shape[1], 8, LANES), jnp.int32),
-            jax.ShapeDtypeStruct(lags.shape, lags.dtype),
-        ),
-        in_specs=[HBM] * 4,
-        out_specs=(VMEM,) * 4,
-        scratch_shapes=[
-            pltpu.VMEM(bank.shape, bank.dtype),
-            pltpu.VMEM(owners.shape, owners.dtype),
-            pltpu.VMEM((rows, LANES), jnp.float32),
-            pltpu.SemaphoreType.DMA((4,)),
-        ],
-        compiler_params=LIMIT,
-        name="pack",
-        cost_estimate=pl.CostEstimate(flops=40_000_000, bytes_accessed=200_000, transcendentals=0),
-    )(*(pltpu.with_memory_space_constraint(x, pltpu.HBM) for x in (bank, data, owners, lags)))
-
-
-def pick_kernel(owners_ref, seen_ref, out_ref):
-    seen = seen_ref[...].astype(jnp.float32)
-    _, groups, _ = seen.shape
-    block = lax.broadcasted_iota(jnp.int32, seen.shape, 0)
-    rows = []
-    for b in range(owners_ref.shape[0]):
-        chosen = block == owners_ref[b, :groups, :][None]
-        rows.append(jnp.sum(jnp.where(chosen, seen, 0.0), axis=0))
-    chunk = jnp.concatenate(rows, axis=0).astype(out_ref.dtype)
+    chunk = wide_ref[...].astype(out_ref.dtype)
     out_ref[...] = jnp.broadcast_to(chunk[None], out_ref.shape)
 
 
-def pick(owners, seen):
-    blocks, groups, lanes = seen.shape
-    return pl.pallas_call(
-        pick_kernel,
-        out_shape=jax.ShapeDtypeStruct((blocks, owners.shape[0] * groups, lanes), seen.dtype),
+def repack(owners, seen, place, peers):
+    batch_count = owners.shape[0]
+    rows = batch_count * seen.shape[2] * (place.shape[2] // LANES)
+    return pl.pallas_call(
+        repack_kernel,
+        out_shape=jax.ShapeDtypeStruct((peers, rows, LANES), seen.dtype),
+        in_specs=[VMEM] * 3,
+        out_specs=VMEM,
+        scratch_shapes=[pltpu.VMEM((rows, LANES), jnp.float32)],
+        compiler_params=LIMIT,
+        name="repack",
+        cost_estimate=pl.CostEstimate(flops=8_000_000, bytes_accessed=500_000, transcendentals=0),
+    )(owners, seen, place)
+
+
+def pick_kernel(inner, owners_ref, seen_ref, out_ref):
+    batch_count = owners_ref.shape[0]
+    rows = seen_ref.shape[1] // batch_count
+    picked = []
+    for b in range(batch_count):
+        owner = owners_ref[b, 0:1, 0:1] // inner
+        picked.append(chosen_source(seen_ref[:, b * rows : (b + 1) * rows].astype(jnp.float32), owner[None]))
+    chunk = jnp.concatenate(picked, axis=0).astype(out_ref.dtype)
+    out_ref[...] = jnp.broadcast_to(chunk[None], out_ref.shape)
+
+
+def pick(owners, seen, inner):
+    return pl.pallas_call(
+        lambda *refs: pick_kernel(inner, *refs),
+        out_shape=jax.ShapeDtypeStruct((inner,) + seen.shape[1:], seen.dtype),
         in_specs=[VMEM, VMEM],
         out_specs=VMEM,
         compiler_params=LIMIT,
@@ -171,8 +191,7 @@
 def stack_kernel(taps_count, tmpl_ref, hankel_ref, scale_ref, lag_ref, out_ref, wide_ref):
     tmpl_count, batch_count, stretch_len = out_ref.shape
     local_sta = hankel_ref.shape[0]
-    groups = tmpl_ref.shape[1] // batch_count
-    inner = batch_count * groups
+    groups = tmpl_ref.shape[1] // (batch_count * local_sta)
     tiles = stretch_len // 128
     lane = lax.broadcasted_iota(jnp.int32, (batch_count * tmpl_count, 128), 1)
     wide_ref[...] = tmpl_ref[...].astype(jnp.float32).reshape(wide_ref.shape)
@@ -181,8 +200,8 @@
         taps = []
         for group in range(groups):
             for batch in range(batch_count):
-                start = sta * inner + batch * groups + group
-                taps.append(wide_ref[pl.ds(start, tmpl_count, stride=local_sta * inner), :])
+                start = (batch * local_sta + sta) * groups + group
+                taps.append(wide_ref[pl.ds(start, tmpl_count, stride=tmpl_ref.shape[1]), :])
         left = jnp.concatenate(taps, axis=0)
         rows = batch_count * tmpl_count
         power = sum(left[g * rows : (g + 1) * rows] * left[g * rows : (g + 1) * rows] for g in range(groups))
@@ -219,14 +238,20 @@
     span_len = bank.shape[-1]
     tmpl_count = bank.shape[1]
     batch_count = owners.shape[0]
-    blocks = lax.axis_size("tm")
+    outer = lax.axis_size("tm") // tmpl_count
+    near = [[far * tmpl_count + i for i in range(tmpl_count)] for far in range(outer)]
+    across = [[far * tmpl_count + i for far in range(outer)] for i in range(tmpl_count)]
+
+    def exchange(value, groups):
+        return lax.all_to_all(value, "tm", 0, 0, axis_index_groups=groups, tiled=True)
+
     source = jnp.transpose(data, (1, 0, 2))
     lags = moveouts.reshape(batch_count * tmpl_count, local_sta)
-    slot, series, owned, lags = pack(jnp.transpose(bank[0], (0, 2, 1, 3)), source, owners[None], lags)
-    seen = lax.all_to_all(slot.reshape(blocks, -1, LANES), "tm", 0, 0, tiled=True)
+    seen = exchange(jnp.transpose(bank[0], (0, 2, 1, 3)), near)
+    series, owned, lags, place = load(source, owners[None], lags, span_len)
     edge = passed_along(source, "tm", -1)
-    chosen = pick(owned, seen)
-    tmpl = lax.all_to_all(chosen, "tm", 0, 0, tiled=True)
+    seen = exchange(repack(owned, seen, place, outer), across)
+    tmpl = exchange(pick(owned, seen, tmpl_count), near)
     hankel, scale = records(series, edge, span_len)
     partial_sum = stack(
         tmpl, hankel, scale, lags, comp_count * span_len, (tmpl_count, batch_count, stretch_len)

time: 62.5 us -> 64.3 us (1.029); the launches traced: 62.3 us -> 63.1 us
  blocking collectives: 43.2 us -> 31.8 us
  starting transfers between devices: 6.91 us -> 17.9 us
  waiting for transfers between devices: 7.2 us -> 8.63 us
    all_to_all x1 -> x2, starting transfers between devices: 4.43 us -> 15.9 us  [exchange(): lax.all_to_all(value, 'tm', 0, 0, axis_index_groups=groups, tiled=True)]
    all_to_all x1, blocking collectives: 24.5 us -> 13.2 us  [exchange(): lax.all_to_all(value, 'tm', 0, 0, axis_index_groups=groups, tiled=True)]
    all_to_all x1 -> x2, waiting for transfers between devices: 3.86 us -> 4.63 us  [exchange(): lax.all_to_all(value, 'tm', 0, 0, axis_index_groups=groups, tiled=True)]
    ppermute x1, waiting for transfers between devices: 3.34 us -> 4 us  [passed_along(): return lax.ppermute(block, axis, route)]
    pallas_call x2 -> x3, Pallas kernels: 1.97 us -> 1.71 us  [the longest x1 0.77 us: load(): pl.pallas_call(load_kernel, out_shape=(jax.ShapeDtypeStruct(data.shape, d...]
  transfers between devices with their start and end apart: 2 -> 3, of which waited for: 2 -> 2; matrix products, arithmetic and copies ran while one was open for 0% -> 0% of each run, Pallas kernels for 2% -> 3%
where the time goes in v3:
time: 64.3 us; the launch traced here: 63.1 us
  blocking collectives  31.8 us (49%)
  starting transfers between devices  17.9 us (28%)
  waiting for transfers between devices  8.63 us (13%)
  Pallas kernels  4.1 us (6%)
    all_to_all x1, blocking collectives, shards(): pieces = lax.all_to_all(partial_sum, 'sta', 0, 0, tiled=True)  18.6 us
    all_to_all x2, starting transfers between devices, exchange(): lax.all_to_all(value, 'tm', 0, 0, axis_index_groups=groups, tiled=True)  15.9 us
    all_to_all x1, blocking collectives, exchange(): lax.all_to_all(value, 'tm', 0, 0, axis_index_groups=groups, tiled=True)  13.2 us
    all_to_all x2, waiting for transfers between devices, exchange(): lax.all_to_all(value, 'tm', 0, 0, axis_index_groups=groups, tiled=True)  4.63 us
    ppermute x1, waiting for transfers between devices, passed_along(): return lax.ppermute(block, axis, route)  4 us
    ppermute x1, starting transfers between devices, passed_along(): return lax.ppermute(block, axis, route)  2.02 us
    pallas_call x1, Pallas kernels, records(): pl.pallas_call(lambda *refs: records_kernel(span_len, *refs), out_shape=(...  1.36 us
  transfers between devices with their start and end apart: 3, of which 2 were waited for; matrix products, arithmetic and copies ran while one was open for 0% of the time, Pallas kernels for 3%

profile of v3, /device:TPU:1, one launch (start us, length us, event | category | flops | bytes accessed | tf_op | source)
XLA Modules:
  0.0 63.1 jit_solution(13505769465202857907)
XLA Ops:
  0.0 0.0 copy-start
  0.0 10.2 %all-to-all-start = ((bf16[8,3,8,150]{3,2,1,0:T(8,128)(2,1)}), bf16[8,3,8,150]{3,2,1,0:T(8,128)(2,1)S(1)}, u32[]{:S(2)}, u32[]{:S(2)}) async-start(bf16[8,3,8,150]{3,2,1,0:T(8,128)(2,1)} %bitcast.6), calls=%async_computation | async-start | bytes 196608 | tf_op jit(solution)/shard_map/all_to_all | solution.py:246
  10.2 0.8 %load.1 = (bf16[3,8,384]{2,1,0:T(8,128)(2,1)S(1)}, s32[2,8,128]{2,1,0:T(8,128)S(1)}, s32[16,8]{1,0:T(8,128)S(1)}, bf16[3,150,512]{2,1,0:T(8,128)(2,1)S(1)}) custom-call(bf16[3,8,384]{2,1,0:T(8,128)(2,1)} %bitcast.7, s32[1,2]{1,0:T(1,128)} %bitcast.10, s32[16,8]{1,0:T(8,128)} %bitcast.9), custom_call_target="tpu_custom_call" | custom-call | flops 500000 | bytes 500000 | tf_op jit(solution)/shard_map/load/pallas_call | solution.py:58
  11.0 4.6 %all-to-all-done.seen_ref = bf16[8,3,8,150]{3,2,1,0:T(8,128)(2,1)S(1)} async-done(((bf16[8,3,8,150]{3,2,1,0:T(8,128)(2,1)}), bf16[8,3,8,150]{3,2,1,0:T(8,128)(2,1)S(1)}, u32[]{:S(2)}, u32[]{:S(2)}) %all-to-all-start) | async-done | bytes 57632 | tf_op jit(solution)/shard_map/all_to_all | solution.py:246
  15.6 0.2 repack.1
  15.9 13.2 %all_to_all.20.refs_1_ = bf16[8,64,128]{2,1,0:T(8,128)(2,1)S(1)} all-to-all(bf16[8,64,128]{2,1,0:T(8,128)(2,1)S(1)} %repack.1), channel_id=1, replica_groups={{0,64,128,192,256,320,384,448},{8,72,136,200,264,328,392,456},{16,80,14..., dimensions={0} | all-to-all | bytes 262144 | tf_op jit(solution)/shard_map/all_to_all | solution.py:246
  29.0 0.7 %pick.1 = bf16[8,64,128]{2,1,0:T(8,128)(2,1)} custom-call(s32[2,8,128]{2,1,0:T(8,128)S(1)} %get-tuple-element.11.owners_ref.refs_0_, bf16[8,64,128]{2,1,0:T(8,128)(2,1)S(1)} %all_to_all.20.refs_1_), custom_call_target="tpu_custom_call" | custom-call | flops 100000 | bytes 200000 | tf_op jit(solution)/shard_map/pick/pallas_call | solution.py:127
  29.8 5.6 %all-to-all-start.2 = ((bf16[8,64,128]{2,1,0:T(8,128)(2,1)}), bf16[8,64,128]{2,1,0:T(8,128)(2,1)S(1)}, u32[]{:S(2)}, u32[]{:S(2)}) async-start(bf16[8,64,128]{2,1,0:T(8,128)(2,1)} %pick.1), calls=%async_computation.2 | async-start | bytes 262144 | tf_op jit(solution)/shard_map/all_to_all | solution.py:246
  35.4 0.0 copy-done
  35.4 2.0 %collective-permute-start = (bf16[3,8,384]{2,1,0:T(8,128)(2,1)S(1)}, bf16[3,8,384]{2,1,0:T(8,128)(2,1)S(1)}, u32[]{:S(2)}, u32[]{:S(2)}) collective-permute-start(bf16[3,8,384]{2,1,0:T(8,128)(2,1)S(1)} %bitcast.8), channel_id=1, source_target_pairs={{8,0},{16,8},{24,16},{32,24},{40,32},{48,40},{56,48},{64,56},{72,6... | collective-permute-start | bytes 55304 | tf_op jit(solution)/shard_map/ppermute | solution.py:23
  37.4 4.0 %collective-permute-done.refs_1_ = bf16[3,8,384]{2,1,0:T(8,128)(2,1)S(1)} collective-permute-done((bf16[3,8,384]{2,1,0:T(8,128)(2,1)S(1)}, bf16[3,8,384]{2,1,0:T(8,128)(2,1)S(1)}, u32[]{:S(2)}, u32[]{:S(2)}) %collective-permute-start) | collective-permute-done | bytes 18464 | tf_op jit(solution)/shard_map/ppermute | solution.py:23
  41.4 1.4 %records.1 = (bf16[8,128,640]{2,1,0:T(8,128)(2,1)S(1)}, f32[8,640]{1,0:T(8,128)S(1)}) custom-call(bf16[3,8,384]{2,1,0:T(8,128)(2,1)S(1)} %get-tuple-element.13.refs_0_, bf16[3,8,384]{2,1,0:T(8,128)(2,1)S(1)} %collective-permute-done.refs_1_), custom_call_target="tpu_custom_call" | custom-call | flops 8000000 | bytes 4000000 | tf_op jit(solution)/shard_map/records/pallas_call | solution.py:177
  42.8 0.0 all-to-all-done.2.refs_0_
  42.8 1.0 %stack.1 = f32[8,2,384]{2,1,0:T(2,128)S(1)} custom-call(bf16[8,64,128]{2,1,0:T(8,128)(2,1)S(1)} %all-to-all-done.2.refs_0_, bf16[8,128,640]{2,1,0:T(8,128)(2,1)S(1)} %get-tuple-element.14.refs_1_, f32[8,640]{1,0:T(8,128)S(1)} %get-tuple-element.15.refs_2_, s32[16,8]{1,0:T(8,128)S(1)} %get-tuple-element.16.refs_3_), custom_call_target="tpu_custom_call" | custom-call | flops 60000000 | bytes 4000000 | tf_op jit(solution)/shard_map/stack/pallas_call | solution.py:224
  43.9 18.6 %all_to_all.21 = f32[8,2,384]{2,1,0:T(2,128)S(1)} all-to-all(f32[8,2,384]{2,1,0:T(2,128)S(1)} %stack.1), channel_id=1, replica_groups=mesh['tm'=64,'sta'=8] {'sta'}, dimensions={0} | all-to-all | bytes 49152 | tf_op jit(solution)/shard_map/all_to_all | solution.py:259
  62.5 0.6 broadcast_in_dim.7
  (1 shorter events, 0.0 us)
Async XLA Ops:
  0.0 35.4 %copy-start = (bf16[8,3,384]{2,0,1:T(8,128)(2,1)S(1)}, bf16[8,3,384]{2,0,1:T(8,128)(2,1)}, u32[]{:S(2)}) copy-start(bf16[8,3,384]{2,0,1:T(8,128)(2,1)} %param.4) | copy-start | bytes 55300
  0.0 15.6 %all-to-all-start = ((bf16[8,3,8,150]{3,2,1,0:T(8,128)(2,1)}), bf16[8,3,8,150]{3,2,1,0:T(8,128)(2,1)S(1)}, u32[]{:S(2)}, u32[]{:S(2)}) async-start(bf16[8,3,8,150]{3,2,1,0:T(8,128)(2,1)} %bitcast.6), calls=%async_computation | async-start | bytes 196608 | tf_op jit(solution)/shard_map/all_to_all | solution.py:246
  29.8 13.0 %all-to-all-start.2 = ((bf16[8,64,128]{2,1,0:T(8,128)(2,1)}), bf16[8,64,128]{2,1,0:T(8,128)(2,1)S(1)}, u32[]{:S(2)}, u32[]{:S(2)}) async-start(bf16[8,64,128]{2,1,0:T(8,128)(2,1)} %pick.1), calls=%async_computation.2 | async-start | bytes 262144 | tf_op jit(solution)/shard_map/all_to_all | solution.py:246
  35.4 6.0 %collective-permute-start = (bf16[3,8,384]{2,1,0:T(8,128)(2,1)S(1)}, bf16[3,8,384]{2,1,0:T(8,128)(2,1)S(1)}, u32[]{:S(2)}, u32[]{:S(2)}) collective-permute-start(bf16[3,8,384]{2,1,0:T(8,128)(2,1)S(1)} %bitcast.8), channel_id=1, source_target_pairs={{8,0},{16,8},{24,16},{32,24},{40,32},{48,40},{56,48},{64,56},{72,6... | collective-permute-start | bytes 55304 | tf_op jit(solution)/shard_map/ppermute | solution.py:23

commit v4 on v2

v4 whole, which is shorter than its diff:
```python
import jax
import jax.numpy as jnp
from jax import lax
from jax.experimental import pallas as pl
from jax.experimental.pallas import tpu as pltpu
from jax.sharding import Mesh, PartitionSpec as P

STEP = 40
LANES = 128

eps = 1e-06

VMEM = pl.BlockSpec(memory_space=pltpu.VMEM)
HBM = pl.BlockSpec(memory_space=pltpu.HBM)
LIMIT = pltpu.CompilerParams(vmem_limit_bytes=24 * 1024 * 1024)


def up_to(value, unit):
    return -(-value // unit) * unit


def turn(value, source):
    return jnp.take_along_axis(value, source & 127, axis=1, mode="promise_in_bounds")


def chosen_source(seen, source):
    block = lax.broadcasted_iota(jnp.int32, seen.shape, 0)
    return jnp.sum(jnp.where(block == source, seen, 0.0), axis=0)


def pack_kernel(bank_hbm, data_hbm, owners_hbm, lags_hbm, out_ref, owners_ref, lags_ref, bank_ref, data_ref, given_ref, wide_ref, sems):
    moves = [
        pltpu.make_async_copy(bank_hbm, bank_ref, sems.at[0]),
        pltpu.make_async_copy(data_hbm, data_ref, sems.at[1]),
        pltpu.make_async_copy(owners_hbm, given_ref, sems.at[2]),
        pltpu.make_async_copy(lags_hbm, lags_ref, sems.at[3]),
    ]
    for move in moves:
        move.start()
    tmpl_count, comp_count, local_sta, span_len = bank_ref.shape
    tiles = data_ref.shape[2] // LANES
    groups = up_to(span_len, STEP) // STEP
    rows = tmpl_count * local_sta
    height = wide_ref.shape[0] // local_sta
    lag = lax.broadcasted_iota(jnp.int32, (span_len, 1), 0)
    target = (lag // STEP) * LANES + lag % STEP
    lane = lax.broadcasted_iota(jnp.int32, (span_len, groups * LANES), 1)
    places = [
        jnp.where(lane == target + comp * STEP, 1.0, 0.0).astype(jnp.bfloat16) for comp in range(comp_count)
    ]
    for at in range(tmpl_count * groups + comp_count * tiles, height):
        wide_ref[pl.ds(at, local_sta, stride=height), :] = jnp.zeros((local_sta, LANES), jnp.float32)
    moves[0].wait()
    packed = None
    for comp in range(comp_count):
        taps = bank_ref[:, comp].astype(jnp.float32).reshape(rows, span_len).astype(jnp.bfloat16)
        placed = jnp.dot(taps, places[comp], preferred_element_type=jnp.float32)
        packed = placed if packed is None else packed + placed
    for tmpl in range(tmpl_count):
        for group in range(groups):
            piece = packed[tmpl * local_sta : (tmpl + 1) * local_sta, group * LANES : (group + 1) * LANES]
            wide_ref[pl.ds(tmpl * groups + group, local_sta, stride=height), :] = piece
    moves[1].wait()
    for comp in range(comp_count):
        for tile in range(tiles):
            piece = data_ref[comp, :, tile * LANES : (tile + 1) * LANES].astype(jnp.float32)
            at = tmpl_count * groups + comp * tiles + tile
            wide_ref[pl.ds(at, local_sta, stride=height), :] = piece
    out_ref[...] = wide_ref[...].astype(jnp.bfloat16)
    moves[2].wait()
    for b in range(owners_ref.shape[0]):
        owners_ref[b] = jnp.broadcast_to(given_ref[:, b : b + 1], owners_ref.shape[1:])
    moves[3].wait()


def pack(bank, data, owners, lags):
    tmpl_count, comp_count, local_sta, span_len = bank.shape
    groups = up_to(span_len, STEP) // STEP
    height = up_to(tmpl_count * groups + comp_count * data.shape[2] // LANES, 16)
    given = [pltpu.with_memory_space_constraint(x, pltpu.HBM) for x in (bank, data, owners, lags)]
    out, owned, own_lags = pl.pallas_call(
        pack_kernel,
        out_shape=(
            jax.ShapeDtypeStruct((local_sta * height, LANES), jnp.bfloat16),
            jax.ShapeDtypeStruct((owners.shape[1], 8, LANES), jnp.int32),
            jax.ShapeDtypeStruct(lags.shape, lags.dtype),
        ),
        in_specs=[HBM] * 4,
        out_specs=(VMEM,) * 3,
        scratch_shapes=[
            pltpu.VMEM(bank.shape, bank.dtype),
            pltpu.VMEM(data.shape, data.dtype),
            pltpu.VMEM(owners.shape, owners.dtype),
            pltpu.VMEM((local_sta * height, LANES), jnp.float32),
            pltpu.SemaphoreType.DMA((4,)),
        ],
        compiler_params=LIMIT,
        name="pack",
        cost_estimate=pl.CostEstimate(flops=40_000_000, bytes_accessed=200_000, transcendentals=0),
    )(*given)
    return out.reshape(local_sta, height, LANES), owned, own_lags


def forward_kernel(sizes, owners_ref, seen_ref, out_ref):
    template_rows, comp_count, tiles, edge_tiles = sizes
    peers = seen_ref.shape[0]
    seen = seen_ref[:, :template_rows].astype(jnp.float32)
    parts = []
    for b in range(owners_ref.shape[0]):
        parts.append(chosen_source(seen, (owners_ref[b, 0:1, 0:1] % peers)[None]))
    first = seen_ref[0].astype(jnp.float32)
    for comp in range(comp_count):
        at = template_rows + comp * tiles
        parts.append(first[at : at + edge_tiles])
    chunk = jnp.concatenate(parts, axis=0)
    rest = out_ref.shape[1] - chunk.shape[0]
    chunk = jnp.concatenate([chunk, jnp.zeros((rest, LANES), jnp.float32)], axis=0).astype(out_ref.dtype)
    out_ref[...] = jnp.broadcast_to(chunk[None], out_ref.shape)


def forward(owners, seen, peers, sizes):
    template_rows, comp_count, tiles, edge_tiles = sizes
    rows = up_to(owners.shape[0] * template_rows + comp_count * edge_tiles, 8)
    return pl.pallas_call(
        lambda *refs: forward_kernel(sizes, *refs),
        out_shape=jax.ShapeDtypeStruct((peers, rows, LANES), seen.dtype),
        in_specs=[VMEM] * 2,
        out_specs=VMEM,
        compiler_params=LIMIT,
        name="forward",
        cost_estimate=pl.CostEstimate(flops=1_000_000, bytes_accessed=500_000, transcendentals=0),
    )(owners, seen)


def stack_kernel(span_len, sizes, owners_ref, seen_ref, got_ref, lag_ref, out_ref, hankel_ref, tap_ref):
    template_rows, comp_count, tiles, edge_tiles = sizes
    blocks, tmpl_count, batch_count, stretch_len = out_ref.shape
    peers = got_ref.shape[0]
    groups = template_rows // tmpl_count
    rows = batch_count * tmpl_count
    taps_count = comp_count * span_len
    body = blocks * tiles
    held = body + edge_tiles
    near, far = lax.axis_index("near"), lax.axis_index("far")

    at = batch_count * template_rows
    edge = chosen_source(got_ref[:, at:].astype(jnp.float32), far + 1)
    row = lax.broadcasted_iota(jnp.int32, (STEP, LANES), 0)
    lane = lax.broadcasted_iota(jnp.int32, (STEP, LANES), 1)
    spare = jnp.zeros((LANES - comp_count * STEP, LANES), jnp.float32)
    samples = []
    for comp in range(comp_count):
        for_comp = []
        for block in range(blocks):
            at = template_rows + comp * tiles
            for_comp.append(seen_ref[block, at : at + tiles].astype(jnp.float32))
        for_comp.append(edge[comp * edge_tiles : (comp + 1) * edge_tiles])
        samples.append(for_comp)

    def sample_row(comp, tile):
        block, within = (tile // tiles, tile % tiles) if tile < body else (blocks, tile - body)
        return samples[comp][block][within : within + 1]

    later = None
    for tile in range(held - 1, -1, -1):
        turned = [
            turn(jnp.broadcast_to(sample_row(comp, tile), (STEP, LANES)), lane + row) for comp in range(comp_count)
        ]
        block = [
            jnp.where(lane + row < LANES, turned[comp], 0.0 if later is None else later[comp])
            for comp in range(comp_count)
        ]
        hankel_ref[:, tile * LANES : (tile + 1) * LANES] = jnp.concatenate(block + [spare], axis=0).astype(jnp.bfloat16)
        later = turned

    height = up_to(held + 1, 8)
    squares = None
    for comp in range(comp_count):
        series = jnp.concatenate(
            samples[comp] + [jnp.zeros((height - held, LANES), jnp.float32)], axis=0
        )
        squares = series * series if squares is None else squares + series * series
    wide_lane = lax.broadcasted_iota(jnp.int32, (height, LANES), 1)

    def ahead(value, amount):
        if amount >= LANES:
            value, amount = pltpu.roll(value, height - 1, 0), amount - LANES
        if amount == 0:
            return value
        value = pltpu.roll(value, LANES - amount, 1)
        return jnp.where(wide_lane < LANES - amount, value, pltpu.roll(value, height - 1, 0))

    run, total, at, width = squares, None, 0, 1
    while width <= span_len:
        if span_len & width:
            piece = ahead(run, at)
            total = piece if total is None else total + piece
            at += width
        if 2 * width <= span_len:
            run = run + ahead(run, width)
        width *= 2
    scale = 1.0 / jnp.sqrt(total / taps_count + eps)

    for b in range(batch_count):
        got = got_ref[:, b * template_rows : (b + 1) * template_rows].astype(jnp.float32)
        source = owners_ref[b, 0:1, 0:1] // seen_ref.shape[0]
        tap_ref[b * template_rows : (b + 1) * template_rows, :] = chosen_source(got, source[None])
    taps = []
    for group in range(groups):
        for b in range(batch_count):
            taps.append(tap_ref[pl.ds(b * template_rows + group, tmpl_count, stride=groups), :])
    left = jnp.concatenate(taps, axis=0)
    power = sum(left[g * rows : (g + 1) * rows] * left[g * rows : (g + 1) * rows] for g in range(groups))
    power = jnp.sum(power, axis=1, keepdims=True) / taps_count
    gain = 1.0 / (taps_count * jnp.sqrt(power + eps))
    left = left.astype(jnp.bfloat16)

    station = lax.broadcasted_iota(jnp.int32, lag_ref.shape, 1)
    lags = jnp.sum(jnp.where(station == near, lag_ref[...], 0), axis=1, keepdims=True)
    step = lax.broadcasted_iota(jnp.int32, (rows, LANES), 1)
    source = step + lags
    after, after_scores = None, None
    for tile in range(held - 1, -1, -1):
        prods = jnp.dot(left, hankel_ref[:, tile * LANES : (tile + 1) * LANES], preferred_element_type=jnp.float32)
        turned = [prods[:rows]]
        for group in range(1, groups):
            turned.append(pltpu.roll(prods[group * rows : (group + 1) * rows], LANES - group * STEP, 1))
        if tile <= body:
            prod = turned[0]
            for group in range(1, groups):
                prod += jnp.where(step < LANES - group * STEP, turned[group], after[group])
            scores = turn(prod * gain * scale[tile : tile + 1], source)
            if tile < body:
                shifted = jnp.where(source < LANES, scores, after_scores)
                block, within = tile // tiles, tile % tiles
                for b in range(batch_count):
                    out_ref[block, :, b, within * LANES : (within + 1) * LANES] = shifted[b * tmpl_count : (b + 1) * tmpl_count]
            after_scores = scores
        after = turned


def stack(owners, seen, got, lags, span_len, sizes, out_shape):
    template_rows, comp_count, tiles, edge_tiles = sizes
    held = out_shape[0] * tiles + edge_tiles
    return pl.pallas_call(
        lambda *refs: stack_kernel(span_len, sizes, *refs),
        out_shape=jax.ShapeDtypeStruct(out_shape, jnp.float32),
        in_specs=[VMEM] * 4,
        out_specs=VMEM,
        scratch_shapes=[
            pltpu.VMEM((LANES, held * LANES), jnp.bfloat16),
            pltpu.VMEM((owners.shape[0] * template_rows, LANES), jnp.float32),
        ],
        compiler_params=LIMIT,
        name="stack",
        cost_estimate=pl.CostEstimate(flops=60_000_000, bytes_accessed=2_000_000, transcendentals=4096),
    )(owners, seen, got, lags)


def shards(data, bank, owners, moveouts):
    local_sta, comp_count, stretch_len = data.shape
    span_len = bank.shape[-1]
    tmpl_count = bank.shape[1]
    batch_count = owners.shape[0]
    far, near, groups = lax.axis_size("far"), lax.axis_size("near"), lax.axis_size("sta")
    tiles = stretch_len // LANES
    template_rows = tmpl_count * (up_to(span_len, STEP) // STEP)
    sizes = (template_rows, comp_count, tiles, 2)

    def exchange(value, axis):
        return lax.all_to_all(value, axis, 0, 0, tiled=True)

    lags = moveouts.reshape(batch_count * tmpl_count, local_sta)
    slot, owned, lags = pack(jnp.transpose(bank[0], (0, 2, 1, 3)), jnp.transpose(data, (1, 0, 2)), owners[None], lags)
    seen = exchange(slot, "near")
    got = exchange(forward(owned, seen, far, sizes), "far")
    scores = stack(owned, seen, got, lags, span_len, sizes, (near, tmpl_count, batch_count, stretch_len))
    pieces = exchange(scores.reshape(near * groups, batch_count, stretch_len), ("near", "sta"))
    return jnp.sum(pieces, axis=0)[:, None, :]


def solution(mesh):
    blocks, groups = mesh.devices.shape
    near = groups
    split = Mesh(mesh.devices.reshape(blocks // near, near, groups), ("far", "near", "sta"))
    time = ("far", "near")
    placed = (P("sta", None, time), P(time, None, "sta", None, None), P(), P(None, None, "sta"))
    return jax.shard_map(
        shards, mesh=split, in_specs=placed, out_specs=P(None, "sta", time), check_vma=False
    )
```

time: 62.5 us -> 56.8 us (0.909)
  blocking collectives: 43.2 us -> 53.1 us
  waiting for transfers between devices: 7.2 us -> 0 us
  starting transfers between devices: 6.91 us -> 0 us
  Pallas kernels: 4.34 us -> 2.83 us
    all_to_all x2 -> x3, blocking collectives: 43.2 us -> 53.1 us  [exchange(): return lax.all_to_all(value, axis, 0, 0, tiled=True)]
    all_to_all x1 -> x0, starting transfers between devices: 4.43 us -> none  [shards(): tmpl = lax.all_to_all(chosen, 'tm', 0, 0, tiled=True)]
    all_to_all x1 -> x0, waiting for transfers between devices: 3.86 us -> none  [shards(): tmpl = lax.all_to_all(chosen, 'tm', 0, 0, tiled=True)]
    ppermute x1 -> x0, waiting for transfers between devices: 3.34 us -> none  [passed_along(): return lax.ppermute(block, axis, route)]
    ppermute x1 -> x0, starting transfers between devices: 2.48 us -> none  [passed_along(): return lax.ppermute(block, axis, route)]
    pallas_call x4 -> x3, Pallas kernels: 4.34 us -> 2.83 us  [the longest x1 1.51 us: stack(): pl.pallas_call(lambda *refs: stack_kernel(span_len, sizes, *refs), out_sh...]
  transfers between devices with their start and end apart: 2 -> 0, of which waited for: 2 -> 0; matrix products, arithmetic and copies ran while one was open for 0% -> 0% of each run, Pallas kernels for 2% -> 0%
where the time goes in v4:
time: 56.8 us; the launch traced here: 56.6 us
  blocking collectives  53.1 us (93%)
  Pallas kernels  2.83 us (5%)
  local copies, waits for them, and re-layouts  0.58 us (1%)
    all_to_all x3, blocking collectives, exchange(): return lax.all_to_all(value, axis, 0, 0, tiled=True)  53.1 us
    pallas_call x1, Pallas kernels, stack(): pl.pallas_call(lambda *refs: stack_kernel(span_len, sizes, *refs), out_sh...  1.51 us
    pallas_call x1, Pallas kernels, pack(): pl.pallas_call(pack_kernel, out_shape=(jax.ShapeDtypeStruct((local_sta *...  1.26 us

profile of v4, /device:TPU:1, one launch (start us, length us, event | category | flops | bytes accessed | tf_op | source)
XLA Modules:
  0.0 56.6 jit_solution(4052621028192975739)
XLA Ops:
  0.0 1.3 %pack.1 = (bf16[384,128]{1,0:T(8,128)(2,1)S(1)}, s32[2,8,128]{2,1,0:T(8,128)S(1)}, s32[16,8]{1,0:T(8,128)S(1)}) custom-call(bf16[8,3,8,150]{3,2,1,0:T(8,128)(2,1)} %bitcast.10, bf16[3,8,384]{2,1,0:T(8,128)(2,1)} %bitcast.11, s32[1,2]{1,0:T(1,128)} %bitcast.13, s32[16,8]{1,0:T(8,128)} %bitcast.12), custom_call_target="tpu_custom_call" | custom-call | flops 40000000 | bytes 200000 | tf_op jit(solution)/shard_map/pack/pallas_call | solution.py:81
  1.3 14.6 %all_to_all.15.refs_1_ = bf16[8,48,128]{2,1,0:T(8,128)(2,1)S(1)} all-to-all(bf16[8,48,128]{2,1,0:T(8,128)(2,1)S(1)} %bitcast.9), channel_id=1, replica_groups=mesh['far'=8,'near'=8,'sta'=8] {'near'}, dimensions={0} | all-to-all | bytes 196608 | tf_op jit(solution)/shard_map/all_to_all | solution.py:271
  15.8 0.1 forward.1
  15.9 13.9 %all_to_all.16.refs_2_ = bf16[8,72,128]{2,1,0:T(8,128)(2,1)S(1)} all-to-all(bf16[8,72,128]{2,1,0:T(8,128)(2,1)S(1)} %forward.1), channel_id=1, replica_groups=mesh['far'=8,'near'=8,'sta'=8] {'far'}, dimensions={0} | all-to-all | bytes 294912 | tf_op jit(solution)/shard_map/all_to_all | solution.py:271
  29.8 1.5 %stack.1 = f32[8,8,2,384]{3,2,1,0:T(2,128)S(1)} custom-call(s32[2,8,128]{2,1,0:T(8,128)S(1)} %get-tuple-element.8.refs_0_, bf16[8,48,128]{2,1,0:T(8,128)(2,1)S(1)} %all_to_all.15.refs_1_, bf16[8,72,128]{2,1,0:T(8,128)(2,1)S(1)} %all_to_all.16.refs_2_, s32[16,8]{1,0:T(8,128)S(1)} %get-tuple-element.10.refs_3_), custom_call_target="tpu_custom_call" | custom-call | flops 60000000 | bytes 2000000 | tf_op jit(solution)/shard_map/stack/pallas_call | solution.py:245
  31.3 24.6 %all_to_all.17 = f32[64,2,384]{2,1,0:T(2,128)S(1)} all-to-all(f32[64,2,384]{2,1,0:T(2,128)S(1)} %bitcast.8), channel_id=1, replica_groups=mesh['far'=8,'near'=8,'sta'=8] {'near','sta'}, dimensions={0} | all-to-all | bytes 393216 | tf_op jit(solution)/shard_map/all_to_all | solution.py:271
  55.9 0.1 reduce_sum.9
  56.0 0.6 %broadcast_in_dim.7 = f32[2,1,384]{2,1,0:T(1,128)} reshape(f32[2,384]{1,0:T(2,128)S(1)} %reduce_sum.9) | data formatting | bytes 6144 | tf_op jit(solution)/shard_map/broadcast_in_dim | solution.py:279

commit v5 on v4

v5 whole, which is shorter than its diff:
```python
import jax
import jax.numpy as jnp
from jax import lax
from jax.experimental import pallas as pl
from jax.experimental.pallas import tpu as pltpu
from jax.sharding import Mesh, PartitionSpec as P

STEP = 40
LANES = 128

eps = 1e-06

VMEM = pl.BlockSpec(memory_space=pltpu.VMEM)
HBM = pl.BlockSpec(memory_space=pltpu.HBM)
LIMIT = pltpu.CompilerParams(vmem_limit_bytes=24 * 1024 * 1024)


def up_to(value, unit):
    return -(-value // unit) * unit


def turn(value, source):
    return jnp.take_along_axis(value, source & 127, axis=1, mode="promise_in_bounds")


def chosen_source(seen, source):
    block = lax.broadcasted_iota(jnp.int32, seen.shape, 0)
    return jnp.sum(jnp.where(block == source, seen, 0.0), axis=0)


def pack_kernel(halves, bank_hbm, data_hbm, owners_hbm, lags_hbm, out_ref, owners_ref, lags_ref, bank_ref, data_ref, given_ref, wide_ref, sems):
    moves = [
        pltpu.make_async_copy(bank_hbm, bank_ref, sems.at[0]),
        pltpu.make_async_copy(data_hbm, data_ref, sems.at[1]),
        pltpu.make_async_copy(owners_hbm, given_ref, sems.at[2]),
        pltpu.make_async_copy(lags_hbm, lags_ref, sems.at[3]),
    ]
    for move in reversed(moves):
        move.start()
    tmpl_count, comp_count, local_sta, span_len = bank_ref.shape
    tiles = data_ref.shape[2] // LANES
    groups = up_to(span_len, STEP) // STEP
    rows = tmpl_count * local_sta
    height = wide_ref.shape[0] // (local_sta * halves)
    share = tmpl_count // halves
    batch_count = owners_ref.shape[0]

    def put(half, at, value):
        wide_ref[pl.ds(half * height + at, local_sta, stride=halves * height), :] = value

    lag = lax.broadcasted_iota(jnp.int32, (span_len, 1), 0)
    target = (lag // STEP) * LANES + lag % STEP
    lane = lax.broadcasted_iota(jnp.int32, (span_len, groups * LANES), 1)
    places = [
        jnp.where(lane == target + comp * STEP, 1.0, 0.0).astype(jnp.bfloat16) for comp in range(comp_count)
    ]
    for half in range(halves):
        for at in range(share * groups + comp_count * tiles + 1, height):
            put(half, at, jnp.zeros((local_sta, LANES), jnp.float32))
    moves[3].wait()
    given_row = lax.broadcasted_iota(jnp.int32, (batch_count * tmpl_count, LANES), 0)
    given_lane = lax.broadcasted_iota(jnp.int32, (batch_count * tmpl_count, LANES), 1)
    for half in range(halves):
        wanted = (given_lane // share) * tmpl_count + given_lane % share * halves + half
        spread = jnp.where(given_row == wanted, 1.0, 0.0).astype(jnp.bfloat16)
        delays = lax.dot_general(
            lags_ref[...].astype(jnp.bfloat16), spread, (((0,), (0,)), ((), ())), preferred_element_type=jnp.float32
        )
        put(half, share * groups + comp_count * tiles, delays)
    moves[2].wait()
    for b in range(owners_ref.shape[0]):
        owners_ref[b] = jnp.broadcast_to(given_ref[:, b : b + 1], owners_ref.shape[1:])
    moves[0].wait()
    packed = None
    for comp in range(comp_count):
        taps = bank_ref[:, comp].astype(jnp.float32).reshape(rows, span_len).astype(jnp.bfloat16)
        placed = jnp.dot(taps, places[comp], preferred_element_type=jnp.float32)
        packed = placed if packed is None else packed + placed
    for tmpl in range(tmpl_count):
        for group in range(groups):
            piece = packed[tmpl * local_sta : (tmpl + 1) * local_sta, group * LANES : (group + 1) * LANES]
            put(tmpl % halves, tmpl // halves * groups + group, piece)
    moves[1].wait()
    for comp in range(comp_count):
        for tile in range(tiles):
            piece = data_ref[comp, :, tile * LANES : (tile + 1) * LANES].astype(jnp.float32)
            for half in range(halves):
                put(half, share * groups + comp * tiles + tile, piece)
    out_ref[...] = wide_ref[...].astype(jnp.bfloat16)


def pack(bank, data, owners, lags, halves):
    tmpl_count, comp_count, local_sta, span_len = bank.shape
    groups = up_to(span_len, STEP) // STEP
    height = up_to(tmpl_count // halves * groups + comp_count * data.shape[2] // LANES + 1, 8)
    blocks = local_sta * halves
    given = [pltpu.with_memory_space_constraint(x, pltpu.HBM) for x in (bank, data, owners, lags)]
    out, owned = pl.pallas_call(
        lambda *refs: pack_kernel(halves, *refs),
        out_shape=(
            jax.ShapeDtypeStruct((blocks * height, LANES), jnp.bfloat16),
            jax.ShapeDtypeStruct((owners.shape[1], 8, LANES), jnp.int32),
        ),
        in_specs=[HBM] * 4,
        out_specs=(VMEM,) * 2,
        scratch_shapes=[
            pltpu.VMEM(lags.shape, lags.dtype),
            pltpu.VMEM(bank.shape, bank.dtype),
            pltpu.VMEM(data.shape, data.dtype),
            pltpu.VMEM(owners.shape, owners.dtype),
            pltpu.VMEM((blocks * height, LANES), jnp.float32),
            pltpu.SemaphoreType.DMA((4,)),
        ],
        compiler_params=LIMIT,
        name="pack",
        cost_estimate=pl.CostEstimate(flops=40_000_000, bytes_accessed=200_000, transcendentals=0),
    )(*given)
    return out.reshape(blocks, height, LANES), owned


def forward_kernel(sizes, owners_ref, seen_ref, out_ref):
    template_rows, comp_count, tiles, edge_tiles, halves = sizes
    peers = seen_ref.shape[0] // halves
    seen = seen_ref[:, :template_rows].astype(jnp.float32)
    parts = []
    for b in range(owners_ref.shape[0]):
        for half in range(halves):
            parts.append(chosen_source(seen, (owners_ref[b, 0:1, 0:1] % peers * halves + half)[None]))
    for half in range(halves):
        first = seen_ref[half].astype(jnp.float32)
        for comp in range(comp_count):
            at = template_rows + comp * tiles
            parts.append(first[at : at + edge_tiles])
    chunk = jnp.concatenate(parts, axis=0)
    rest = out_ref.shape[1] - chunk.shape[0]
    chunk = jnp.concatenate([chunk, jnp.zeros((rest, LANES), jnp.float32)], axis=0).astype(out_ref.dtype)
    out_ref[...] = jnp.broadcast_to(chunk[None], out_ref.shape)


def forward(owners, seen, peers, sizes):
    template_rows, comp_count, tiles, edge_tiles, halves = sizes
    rows = up_to(halves * (owners.shape[0] * template_rows + comp_count * edge_tiles), 8)
    return pl.pallas_call(
        lambda *refs: forward_kernel(sizes, *refs),
        out_shape=jax.ShapeDtypeStruct((peers, rows, LANES), seen.dtype),
        in_specs=[VMEM] * 2,
        out_specs=VMEM,
        compiler_params=LIMIT,
        name="forward",
        cost_estimate=pl.CostEstimate(flops=1_000_000, bytes_accessed=500_000, transcendentals=0),
    )(owners, seen)


def stack_kernel(span_len, sizes, owners_ref, seen_ref, got_ref, out_ref, hankel_ref, tap_ref, score_ref):
    template_rows, comp_count, tiles, edge_tiles, halves = sizes
    blocks, tmpl_count, batch_count, stretch_len = out_ref.shape
    groups = template_rows // tmpl_count
    rows = batch_count * tmpl_count
    taps_count = comp_count * span_len
    body = blocks * tiles
    held = body + edge_tiles
    at = halves * batch_count * template_rows
    edges = chosen_source(got_ref[:, at:].astype(jnp.float32), lax.axis_index("far") + 1)
    def station_samples(half):
        samples = []
        for comp in range(comp_count):
            at = template_rows + comp * tiles
            parts = [seen_ref[block * halves + half, at : at + tiles].astype(jnp.float32) for block in range(blocks)]
            at = (half * comp_count + comp) * edge_tiles
            samples.append(parts + [edges[at : at + edge_tiles]])
        return samples

    def build_hankel(all_samples):
        for half in range(halves):
            hankel_ref[half, comp_count * STEP :, :] = jnp.zeros((LANES - comp_count * STEP, held * LANES), jnp.bfloat16)
        row = lax.broadcasted_iota(jnp.int32, (8, LANES), 0)
        lane = lax.broadcasted_iota(jnp.int32, (8, LANES), 1)
        for lag in range(0, STEP, 8):
            source = lane + row + lag
            for half in range(halves):
                for comp in range(comp_count):
                    at, later = comp * STEP + lag, 0.0
                    for tile in range(held - 1, -1, -1):
                        block, within = (tile // tiles, tile % tiles) if tile < body else (blocks, tile - body)
                        base = all_samples[half][comp][block][within : within + 1]
                        turned = turn(jnp.broadcast_to(base, (8, LANES)), source)
                        value = jnp.where(source < LANES, turned, later).astype(jnp.bfloat16)
                        hankel_ref[half, at : at + 8, tile * LANES : (tile + 1) * LANES] = value
                        later = turned

    height = up_to(held + 1, 8)

    def inverse_energy(all_samples):
        rows = []
        for samples in all_samples:
            squares = None
            for comp in range(comp_count):
                series = jnp.concatenate(samples[comp] + [jnp.zeros((height - held, LANES), jnp.float32)], axis=0)
                squares = series * series if squares is None else squares + series * series
            rows.append(squares)
        first = jnp.concatenate(rows, axis=0)
        total_rows = first.shape[0]
        reach = up_to(LANES + span_len, LANES) // LANES
        sides = [first] + [pltpu.roll(first, total_rows - side, 0) for side in range(1, reach)]
        wide = jnp.concatenate(sides, axis=1)

        def ahead(value, amount):
            return pltpu.roll(value, reach * LANES - amount, 1)[:, : value.shape[1]] if amount else value

        sums, width = {1: wide}, 1
        for factor in (2, 2, 4, 4):
            last = sums[1] if width <= 2 else sums[width]
            unit = 1 if width <= 2 else width
            count = width * factor // unit
            total = last
            for part in range(1, count):
                total = total + ahead(last, part * unit)
            width *= factor
            sums[width] = total
        total, at = None, 0
        for width in sorted(sums, reverse=True):
            while span_len - at >= width:
                piece = ahead(sums[width], at)[:, :LANES]
                total = piece if total is None else total + piece
                at += width
        scale = 1.0 / jnp.sqrt(total / taps_count + eps)
        return [scale[i * height : (i + 1) * height] for i in range(len(all_samples))]

    for b in range(batch_count):
        at = b * halves * template_rows
        got = got_ref[:, at : at + halves * template_rows].astype(jnp.float32)
        source = owners_ref[b, 0:1, 0:1] // blocks
        tap_ref[at : at + halves * template_rows, :] = chosen_source(got, source[None])
    step = lax.broadcasted_iota(jnp.int32, (rows, LANES), 1)
    slot = lax.broadcasted_iota(jnp.int32, (rows, LANES), 0)
    lefts, gains, sources = [], [], []
    all_samples = [station_samples(half) for half in range(halves)]
    scales = inverse_energy(all_samples)
    build_hankel(all_samples)
    for half in range(halves):
        taps = []
        for group in range(groups):
            for b in range(batch_count):
                start = (b * halves + half) * template_rows + group
                taps.append(tap_ref[pl.ds(start, tmpl_count, stride=groups), :])
        left = jnp.concatenate(taps, axis=0)
        power = sum(left[g * rows : (g + 1) * rows] * left[g * rows : (g + 1) * rows] for g in range(groups))
        power = jnp.sum(power, axis=1, keepdims=True) / taps_count
        gains.append(1.0 / (taps_count * jnp.sqrt(power + eps)))
        lefts.append(left.astype(jnp.bfloat16))
        at = template_rows + comp_count * tiles
        delays = jnp.broadcast_to(seen_ref[half, at : at + 1].astype(jnp.float32), (rows, LANES))
        lags = jnp.sum(jnp.where(step == slot, delays, 0.0), axis=1, keepdims=True)
        sources.append(step + lags.astype(jnp.int32))
    for half in range(halves):
        prods = jnp.dot(lefts[half], hankel_ref[half], preferred_element_type=jnp.float32)
        after = None
        for tile in range(held - 1, -1, -1):
            at = tile * LANES
            turned = [prods[:rows, at : at + LANES]]
            for group in range(1, groups):
                part = prods[group * rows : (group + 1) * rows, at : at + LANES]
                turned.append(pltpu.roll(part, LANES - group * STEP, 1))
            if tile <= body:
                prod = turned[0]
                for group in range(1, groups):
                    prod += jnp.where(step < LANES - group * STEP, turned[group], after[group])
                score_ref[half, :, at : at + LANES] = prod * gains[half] * scales[half][tile : tile + 1]
            after = turned
    totals = [None] * body
    for half in range(halves):
        later = None
        for tile in range(body, -1, -1):
            scores = turn(score_ref[half, :, tile * LANES : (tile + 1) * LANES], sources[half])
            if tile < body:
                shifted = jnp.where(sources[half] < LANES, scores, later)
                totals[tile] = shifted if half == 0 else totals[tile] + shifted
            later = scores
    for tile in range(body):
        block, within = tile // tiles, tile % tiles
        for b in range(batch_count):
            part = totals[tile][b * tmpl_count : (b + 1) * tmpl_count]
            out_ref[block, :, b, within * LANES : (within + 1) * LANES] = part


def stack(owners, seen, got, span_len, sizes, out_shape):
    template_rows, comp_count, tiles, edge_tiles, halves = sizes
    held = out_shape[0] * tiles + edge_tiles
    return pl.pallas_call(
        lambda *refs: stack_kernel(span_len, sizes, *refs),
        out_shape=jax.ShapeDtypeStruct(out_shape, jnp.float32),
        in_specs=[VMEM] * 3,
        out_specs=VMEM,
        scratch_shapes=[
            pltpu.VMEM((halves, LANES, held * LANES), jnp.bfloat16),
            pltpu.VMEM((owners.shape[0] * halves * template_rows, LANES), jnp.float32),
            pltpu.VMEM((halves, out_shape[1] * out_shape[2], held * LANES), jnp.float32),
        ],
        compiler_params=LIMIT,
        name="stack",
        cost_estimate=pl.CostEstimate(flops=60_000_000, bytes_accessed=2_000_000, transcendentals=4096),
    )(owners, seen, got)


def shards(data, bank, owners, moveouts):
    local_sta, comp_count, stretch_len = data.shape
    span_len = bank.shape[-1]
    tmpl_count = bank.shape[1]
    batch_count = owners.shape[0]
    far, near, across, halves = (lax.axis_size(axis) for axis in ("far", "near", "across", "half"))
    tiles = stretch_len // LANES
    share = tmpl_count // halves
    sizes = (share * (up_to(span_len, STEP) // STEP), comp_count, tiles, 2, halves)

    def exchange(value, axis):
        return lax.all_to_all(value, axis, 0, 0, tiled=True)

    lags = moveouts.reshape(batch_count * tmpl_count, local_sta)
    slot, owned = pack(jnp.transpose(bank[0], (0, 2, 1, 3)), jnp.transpose(data, (1, 0, 2)), owners[None], lags, halves)
    seen = exchange(slot, ("near", "half"))
    got = exchange(forward(owned, seen, far, sizes), "far")
    scores = stack(owned, seen, got, span_len, sizes, (near, share, batch_count, stretch_len))
    pieces = exchange(scores.reshape(near * across, batch_count, stretch_len), ("near", "across"))
    return jnp.sum(pieces, axis=0)[:, None, :]


def solution(mesh):
    blocks, groups = mesh.devices.shape
    near, halves = 8, 2
    shape = (blocks // near, near, groups // halves, halves)
    split = Mesh(mesh.devices.reshape(shape), ("far", "near", "across", "half"))
    time, sta = ("far", "near"), ("across", "half")
    placed = (P(sta, None, time), P(time, None, sta, None, None), P(), P(None, None, sta))
    return jax.shard_map(
        shards, mesh=split, in_specs=placed, out_specs=P(None, sta, time), check_vma=False
    )
```

time: 56.8 us -> 54.4 us (0.958)
  blocking collectives: 53.1 us -> 50.5 us
    all_to_all x3, blocking collectives: 53.1 us -> 50.5 us  [exchange(): return lax.all_to_all(value, axis, 0, 0, tiled=True)]
where the time goes in v5:
time: 54.4 us; the launch traced here: 54.2 us
  blocking collectives  50.5 us (93%)
  Pallas kernels  3 us (6%)
  local copies, waits for them, and re-layouts  0.58 us (1%)
    all_to_all x3, blocking collectives, exchange(): return lax.all_to_all(value, axis, 0, 0, tiled=True)  50.5 us
    pallas_call x1, Pallas kernels, stack(): pl.pallas_call(lambda *refs: stack_kernel(span_len, sizes, *refs), out_sh...  1.56 us
    pallas_call x1, Pallas kernels, pack(): pl.pallas_call(lambda *refs: pack_kernel(halves, *refs), out_shape=(jax.S...  1.35 us

profile of v5, /device:TPU:1, one launch (start us, length us, event | category | flops | bytes accessed | tf_op | source)
XLA Modules:
  0.0 54.2 jit_solution(13561327791905771958)
XLA Ops:
  0.0 1.3 %pack.1 = (bf16[512,128]{1,0:T(8,128)(2,1)S(1)}, s32[2,8,128]{2,1,0:T(8,128)S(1)}) custom-call(bf16[8,3,8,150]{3,2,1,0:T(8,128)(2,1)} %bitcast.10, bf16[3,8,384]{2,1,0:T(8,128)(2,1)} %bitcast.11, s32[1,2]{1,0:T(1,128)} %bitcast.13, s32[16,8]{1,0:T(8,128)} %bitcast.12), custom_call_target="tpu_custom_call" | custom-call | flops 40000000 | bytes 200000 | tf_op jit(solution)/shard_map/pack/pallas_call | solution.py:98
  1.4 20.6 %all_to_all.15.refs_1_ = bf16[16,32,128]{2,1,0:T(8,128)(2,1)S(1)} all-to-all(bf16[16,32,128]{2,1,0:T(8,128)(2,1)S(1)} %bitcast.9), channel_id=1, replica_groups=mesh['far'=8,'near'=8,'across'=4,'half'=2] {'near','half'}, dimensions={0} | all-to-all | bytes 262144 | tf_op jit(solution)/shard_map/all_to_all | solution.py:316
  21.9 0.1 forward.1
  22.0 14.7 %all_to_all.16.refs_2_ = bf16[8,80,128]{2,1,0:T(8,128)(2,1)S(1)} all-to-all(bf16[8,80,128]{2,1,0:T(8,128)(2,1)S(1)} %forward.1), channel_id=1, replica_groups=mesh['far'=8,'near'=8,'across'=4,'half'=2] {'far'}, dimensions={0} | all-to-all | bytes 327680 | tf_op jit(solution)/shard_map/all_to_all | solution.py:316
  36.7 1.6 %stack.1 = f32[8,4,2,384]{3,2,1,0:T(2,128)S(1)} custom-call(s32[2,8,128]{2,1,0:T(8,128)S(1)} %get-tuple-element.7.refs_0_, bf16[16,32,128]{2,1,0:T(8,128)(2,1)S(1)} %all_to_all.15.refs_1_, bf16[8,80,128]{2,1,0:T(8,128)(2,1)S(1)} %all_to_all.16.refs_2_), custom_call_target="tpu_custom_call" | custom-call | flops 60000000 | bytes 2000000 | tf_op jit(solution)/shard_map/stack/pallas_call | solution.py:289
  38.3 15.2 %all_to_all.17 = f32[32,2,384]{2,1,0:T(2,128)S(1)} all-to-all(f32[32,2,384]{2,1,0:T(2,128)S(1)} %bitcast.8), channel_id=1, replica_groups=mesh['far'=8,'near'=8,'across'=4,'half'=2] {'near','across'}, dimensions={0} | all-to-all | bytes 196608 | tf_op jit(solution)/shard_map/all_to_all | solution.py:316
  53.5 0.1 reduce_sum.9
  53.6 0.6 %broadcast_in_dim.7 = f32[2,1,384]{2,1,0:T(1,128)} reshape(f32[2,384]{1,0:T(2,128)S(1)} %reduce_sum.9) | data formatting | bytes 6144 | tf_op jit(solution)/shard_map/broadcast_in_dim | solution.py:324

commit v6 on v5

--- a/solution.py
+++ b/solution.py
@@ -46,7 +46,7 @@
     batch_count = owners_ref.shape[0]
 
     def put(half, at, value):
-        wide_ref[pl.ds(half * height + at, local_sta, stride=halves * height), :] = value
+        wide_ref[pl.ds(half * local_sta * height + at, local_sta, stride=height), :] = value
 
     lag = lax.broadcasted_iota(jnp.int32, (span_len, 1), 0)
     target = (lag // STEP) * LANES + lag % STEP
@@ -70,6 +70,12 @@
     moves[2].wait()
     for b in range(owners_ref.shape[0]):
         owners_ref[b] = jnp.broadcast_to(given_ref[:, b : b + 1], owners_ref.shape[1:])
+    moves[1].wait()
+    for comp in range(comp_count):
+        for tile in range(tiles):
+            piece = data_ref[comp, :, tile * LANES : (tile + 1) * LANES].astype(jnp.float32)
+            for half in range(halves):
+                put(half, share * groups + comp * tiles + tile, piece)
     moves[0].wait()
     packed = None
     for comp in range(comp_count):
@@ -80,12 +86,6 @@
         for group in range(groups):
             piece = packed[tmpl * local_sta : (tmpl + 1) * local_sta, group * LANES : (group + 1) * LANES]
             put(tmpl % halves, tmpl // halves * groups + group, piece)
-    moves[1].wait()
-    for comp in range(comp_count):
-        for tile in range(tiles):
-            piece = data_ref[comp, :, tile * LANES : (tile + 1) * LANES].astype(jnp.float32)
-            for half in range(halves):
-                put(half, share * groups + comp * tiles + tile, piece)
     out_ref[...] = wide_ref[...].astype(jnp.bfloat16)
 
 
@@ -125,9 +125,9 @@
     parts = []
     for b in range(owners_ref.shape[0]):
         for half in range(halves):
-            parts.append(chosen_source(seen, (owners_ref[b, 0:1, 0:1] % peers * halves + half)[None]))
-    for half in range(halves):
-        first = seen_ref[half].astype(jnp.float32)
+            parts.append(chosen_source(seen, (owners_ref[b, 0:1, 0:1] % peers + half * peers)[None]))
+    for half in range(halves):
+        first = seen_ref[half * peers].astype(jnp.float32)
         for comp in range(comp_count):
             at = template_rows + comp * tiles
             parts.append(first[at : at + edge_tiles])
@@ -153,7 +153,7 @@
 
 def stack_kernel(span_len, sizes, owners_ref, seen_ref, got_ref, out_ref, hankel_ref, tap_ref, score_ref):
     template_rows, comp_count, tiles, edge_tiles, halves = sizes
-    blocks, tmpl_count, batch_count, stretch_len = out_ref.shape
+    tmpl_count, blocks, batch_count, stretch_len = out_ref.shape
     groups = template_rows // tmpl_count
     rows = batch_count * tmpl_count
     taps_count = comp_count * span_len
@@ -165,7 +165,7 @@
         samples = []
         for comp in range(comp_count):
             at = template_rows + comp * tiles
-            parts = [seen_ref[block * halves + half, at : at + tiles].astype(jnp.float32) for block in range(blocks)]
+            parts = [seen_ref[half * blocks + block, at : at + tiles].astype(jnp.float32) for block in range(blocks)]
             at = (half * comp_count + comp) * edge_tiles
             samples.append(parts + [edges[at : at + edge_tiles]])
         return samples
@@ -208,15 +208,9 @@
             return pltpu.roll(value, reach * LANES - amount, 1)[:, : value.shape[1]] if amount else value
 
         sums, width = {1: wide}, 1
-        for factor in (2, 2, 4, 4):
-            last = sums[1] if width <= 2 else sums[width]
-            unit = 1 if width <= 2 else width
-            count = width * factor // unit
-            total = last
-            for part in range(1, count):
-                total = total + ahead(last, part * unit)
-            width *= factor
-            sums[width] = total
+        while 2 * width <= min(span_len, LANES // 2):
+            sums[2 * width] = sums[width] + ahead(sums[width], width)
+            width *= 2
         total, at = None, 0
         for width in sorted(sums, reverse=True):
             while span_len - at >= width:
@@ -249,7 +243,7 @@
         gains.append(1.0 / (taps_count * jnp.sqrt(power + eps)))
         lefts.append(left.astype(jnp.bfloat16))
         at = template_rows + comp_count * tiles
-        delays = jnp.broadcast_to(seen_ref[half, at : at + 1].astype(jnp.float32), (rows, LANES))
+        delays = jnp.broadcast_to(seen_ref[half * blocks, at : at + 1].astype(jnp.float32), (rows, LANES))
         lags = jnp.sum(jnp.where(step == slot, delays, 0.0), axis=1, keepdims=True)
         sources.append(step + lags.astype(jnp.int32))
     for half in range(halves):
@@ -280,12 +274,12 @@
         block, within = tile // tiles, tile % tiles
         for b in range(batch_count):
             part = totals[tile][b * tmpl_count : (b + 1) * tmpl_count]
-            out_ref[block, :, b, within * LANES : (within + 1) * LANES] = part
+            out_ref[:, block, b, within * LANES : (within + 1) * LANES] = part
 
 
 def stack(owners, seen, got, span_len, sizes, out_shape):
     template_rows, comp_count, tiles, edge_tiles, halves = sizes
-    held = out_shape[0] * tiles + edge_tiles
+    held = out_shape[1] * tiles + edge_tiles
     return pl.pallas_call(
         lambda *refs: stack_kernel(span_len, sizes, *refs),
         out_shape=jax.ShapeDtypeStruct(out_shape, jnp.float32),
@@ -294,7 +288,7 @@
         scratch_shapes=[
             pltpu.VMEM((halves, LANES, held * LANES), jnp.bfloat16),
             pltpu.VMEM((owners.shape[0] * halves * template_rows, LANES), jnp.float32),
-            pltpu.VMEM((halves, out_shape[1] * out_shape[2], held * LANES), jnp.float32),
+            pltpu.VMEM((halves, out_shape[0] * out_shape[2], held * LANES), jnp.float32),
         ],
         compiler_params=LIMIT,
         name="stack",
@@ -317,10 +311,10 @@
 
     lags = moveouts.reshape(batch_count * tmpl_count, local_sta)
     slot, owned = pack(jnp.transpose(bank[0], (0, 2, 1, 3)), jnp.transpose(data, (1, 0, 2)), owners[None], lags, halves)
-    seen = exchange(slot, ("near", "half"))
+    seen = exchange(slot, ("half", "near"))
     got = exchange(forward(owned, seen, far, sizes), "far")
-    scores = stack(owned, seen, got, span_len, sizes, (near, share, batch_count, stretch_len))
-    pieces = exchange(scores.reshape(near * across, batch_count, stretch_len), ("near", "across"))
+    scores = stack(owned, seen, got, span_len, sizes, (share, near, batch_count, stretch_len))
+    pieces = exchange(scores.reshape(near * across, batch_count, stretch_len), ("across", "near"))
     return jnp.sum(pieces, axis=0)[:, None, :]
 
 

time: 54.4 us -> 54.4 us (level)
  no operation moved by 1% of the time
where the time goes in v6:
time: 54.4 us; the launch traced here: 54.1 us
  blocking collectives  50.7 us (93%)
  Pallas kernels  2.8 us (5%)
  local copies, waits for them, and re-layouts  0.58 us (1%)
    all_to_all x3, blocking collectives, exchange(): return lax.all_to_all(value, axis, 0, 0, tiled=True)  50.7 us
    pallas_call x1, Pallas kernels, pack(): pl.pallas_call(lambda *refs: pack_kernel(halves, *refs), out_shape=(jax.S...  1.37 us
    pallas_call x1, Pallas kernels, stack(): pl.pallas_call(lambda *refs: stack_kernel(span_len, sizes, *refs), out_sh...  1.34 us

profile of v6, /device:TPU:1, one launch (start us, length us, event | category | flops | bytes accessed | tf_op | source)
XLA Modules:
  0.0 54.1 jit_solution(12296030793233142630)
XLA Ops:
  0.0 1.4 %pack.1 = (bf16[512,128]{1,0:T(8,128)(2,1)S(1)}, s32[2,8,128]{2,1,0:T(8,128)S(1)}) custom-call(bf16[8,3,8,150]{3,2,1,0:T(8,128)(2,1)} %bitcast.10, bf16[3,8,384]{2,1,0:T(8,128)(2,1)} %bitcast.11, s32[1,2]{1,0:T(1,128)} %bitcast.13, s32[16,8]{1,0:T(8,128)} %bitcast.12), custom_call_target="tpu_custom_call" | custom-call | flops 40000000 | bytes 200000 | tf_op jit(solution)/shard_map/pack/pallas_call | solution.py:98
  1.4 20.5 %all_to_all.15.refs_1_ = bf16[16,32,128]{2,1,0:T(8,128)(2,1)S(1)} all-to-all(bf16[16,32,128]{2,1,0:T(8,128)(2,1)S(1)} %bitcast.9), channel_id=1, replica_groups=mesh['far'=8,'near'=8,'across'=4,'half'=2] {'half','near'}, dimensions={0} | all-to-all | bytes 262144 | tf_op jit(solution)/shard_map/all_to_all | solution.py:310
  21.9 0.1 forward.1
  22.0 16.8 %all_to_all.16.refs_2_ = bf16[8,80,128]{2,1,0:T(8,128)(2,1)S(1)} all-to-all(bf16[8,80,128]{2,1,0:T(8,128)(2,1)S(1)} %forward.1), channel_id=1, replica_groups=mesh['far'=8,'near'=8,'across'=4,'half'=2] {'far'}, dimensions={0} | all-to-all | bytes 327680 | tf_op jit(solution)/shard_map/all_to_all | solution.py:310
  38.8 1.3 %stack.1 = f32[4,8,2,384]{3,2,1,0:T(2,128)S(1)} custom-call(s32[2,8,128]{2,1,0:T(8,128)S(1)} %get-tuple-element.7.refs_0_, bf16[16,32,128]{2,1,0:T(8,128)(2,1)S(1)} %all_to_all.15.refs_1_, bf16[8,80,128]{2,1,0:T(8,128)(2,1)S(1)} %all_to_all.16.refs_2_), custom_call_target="tpu_custom_call" | custom-call | flops 60000000 | bytes 2000000 | tf_op jit(solution)/shard_map/stack/pallas_call | solution.py:283
  40.1 13.4 %all_to_all.17 = f32[32,2,384]{2,1,0:T(2,128)S(1)} all-to-all(f32[32,2,384]{2,1,0:T(2,128)S(1)} %bitcast.8), channel_id=1, replica_groups=mesh['far'=8,'near'=8,'across'=4,'half'=2] {'across','near'}, dimensions={0} | all-to-all | bytes 196608 | tf_op jit(solution)/shard_map/all_to_all | solution.py:310
  53.5 0.1 reduce_sum.9
  53.6 0.6 %broadcast_in_dim.7 = f32[2,1,384]{2,1,0:T(1,128)} reshape(f32[2,384]{1,0:T(2,128)S(1)} %reduce_sum.9) | data formatting | bytes 6144 | tf_op jit(solution)/shard_map/broadcast_in_dim | solution.py:318

commit v7 on v6

--- a/solution.py
+++ b/solution.py
@@ -30,12 +30,16 @@
 
 def pack_kernel(halves, bank_hbm, data_hbm, owners_hbm, lags_hbm, out_ref, owners_ref, lags_ref, bank_ref, data_ref, given_ref, wide_ref, sems):
     moves = [
-        pltpu.make_async_copy(bank_hbm, bank_ref, sems.at[0]),
+        None,
         pltpu.make_async_copy(data_hbm, data_ref, sems.at[1]),
         pltpu.make_async_copy(owners_hbm, given_ref, sems.at[2]),
         pltpu.make_async_copy(lags_hbm, lags_ref, sems.at[3]),
     ]
-    for move in reversed(moves):
+    pieces = [
+        pltpu.make_async_copy(bank_hbm.at[:, comp], bank_ref.at[:, comp], sems.at[4 + comp])
+        for comp in range(bank_ref.shape[1])
+    ]
+    for move in pieces + moves[:0:-1]:
         move.start()
     tmpl_count, comp_count, local_sta, span_len = bank_ref.shape
     tiles = data_ref.shape[2] // LANES
@@ -76,9 +80,9 @@
             piece = data_ref[comp, :, tile * LANES : (tile + 1) * LANES].astype(jnp.float32)
             for half in range(halves):
                 put(half, share * groups + comp * tiles + tile, piece)
-    moves[0].wait()
     packed = None
     for comp in range(comp_count):
+        pieces[comp].wait()
         taps = bank_ref[:, comp].astype(jnp.float32).reshape(rows, span_len).astype(jnp.bfloat16)
         placed = jnp.dot(taps, places[comp], preferred_element_type=jnp.float32)
         packed = placed if packed is None else packed + placed
@@ -109,7 +113,7 @@
             pltpu.VMEM(data.shape, data.dtype),
             pltpu.VMEM(owners.shape, owners.dtype),
             pltpu.VMEM((blocks * height, LANES), jnp.float32),
-            pltpu.SemaphoreType.DMA((4,)),
+            pltpu.SemaphoreType.DMA((4 + comp_count,)),
         ],
         compiler_params=LIMIT,
         name="pack",

time: 54.4 us -> 54.5 us (level)
  no operation moved by 1% of the time
where the time goes in v7:
time: 54.5 us; the launch traced here: 54.2 us
  blocking collectives  50.7 us (93%)
  Pallas kernels  2.88 us (5%)
  local copies, waits for them, and re-layouts  0.58 us (1%)
    all_to_all x3, blocking collectives, exchange(): return lax.all_to_all(value, axis, 0, 0, tiled=True)  50.7 us
    pallas_call x1, Pallas kernels, pack(): pl.pallas_call(lambda *refs: pack_kernel(halves, *refs), out_shape=(jax.S...  1.45 us
    pallas_call x1, Pallas kernels, stack(): pl.pallas_call(lambda *refs: stack_kernel(span_len, sizes, *refs), out_sh...  1.34 us

profile of v7, /device:TPU:1, one launch (start us, length us, event | category | flops | bytes accessed | tf_op | source)
XLA Modules:
  0.0 54.2 jit_solution(7950902225892792199)
XLA Ops:
  0.0 1.5 %pack.1 = (bf16[512,128]{1,0:T(8,128)(2,1)S(1)}, s32[2,8,128]{2,1,0:T(8,128)S(1)}) custom-call(bf16[8,3,8,150]{3,2,1,0:T(8,128)(2,1)} %bitcast.10, bf16[3,8,384]{2,1,0:T(8,128)(2,1)} %bitcast.11, s32[1,2]{1,0:T(1,128)} %bitcast.13, s32[16,8]{1,0:T(8,128)} %bitcast.12), custom_call_target="tpu_custom_call" | custom-call | flops 40000000 | bytes 200000 | tf_op jit(solution)/shard_map/pack/pallas_call | solution.py:102
  1.5 20.5 %all_to_all.15.refs_1_ = bf16[16,32,128]{2,1,0:T(8,128)(2,1)S(1)} all-to-all(bf16[16,32,128]{2,1,0:T(8,128)(2,1)S(1)} %bitcast.9), channel_id=1, replica_groups=mesh['far'=8,'near'=8,'across'=4,'half'=2] {'half','near'}, dimensions={0} | all-to-all | bytes 262144 | tf_op jit(solution)/shard_map/all_to_all | solution.py:314
  22.0 0.1 forward.1
  22.1 16.8 %all_to_all.16.refs_2_ = bf16[8,80,128]{2,1,0:T(8,128)(2,1)S(1)} all-to-all(bf16[8,80,128]{2,1,0:T(8,128)(2,1)S(1)} %forward.1), channel_id=1, replica_groups=mesh['far'=8,'near'=8,'across'=4,'half'=2] {'far'}, dimensions={0} | all-to-all | bytes 327680 | tf_op jit(solution)/shard_map/all_to_all | solution.py:314
  38.8 1.3 %stack.1 = f32[4,8,2,384]{3,2,1,0:T(2,128)S(1)} custom-call(s32[2,8,128]{2,1,0:T(8,128)S(1)} %get-tuple-element.7.refs_0_, bf16[16,32,128]{2,1,0:T(8,128)(2,1)S(1)} %all_to_all.15.refs_1_, bf16[8,80,128]{2,1,0:T(8,128)(2,1)S(1)} %all_to_all.16.refs_2_), custom_call_target="tpu_custom_call" | custom-call | flops 60000000 | bytes 2000000 | tf_op jit(solution)/shard_map/stack/pallas_call | solution.py:287
  40.2 13.4 %all_to_all.17 = f32[32,2,384]{2,1,0:T(2,128)S(1)} all-to-all(f32[32,2,384]{2,1,0:T(2,128)S(1)} %bitcast.8), channel_id=1, replica_groups=mesh['far'=8,'near'=8,'across'=4,'half'=2] {'across','near'}, dimensions={0} | all-to-all | bytes 196608 | tf_op jit(solution)/shard_map/all_to_all | solution.py:314
  53.6 0.1 reduce_sum.9
  53.6 0.6 %broadcast_in_dim.7 = f32[2,1,384]{2,1,0:T(1,128)} reshape(f32[2,384]{1,0:T(2,128)S(1)} %reduce_sum.9) | data formatting | bytes 6144 | tf_op jit(solution)/shard_map/broadcast_in_dim | solution.py:322
